TPU v7x, 256 devices: a whole 4x4x8 slice. The times are simulated.
256 devices in a mesh: rows: 64 (over z, x, core), coil: 4 (over y).
Axes of the slice: x: 4, y: 4, z: 8, core: 2. Of those that a mesh axis runs over, the one named last changes fastest.
Arguments:
- kspace: float32 [128, 32768], P('coil', 'rows'), may hold values from -6 to 6
- sample_mask: int32 [128, 32768], P('coil', 'rows'), may hold values 0 or 1
- start_basis: float32 [4, 2048, 128], P('coil', 'rows'), may hold values from -6 to 6
Outputs:
- recovered: float32 [128, 32768], P('coil', 'rows')
- basis: float32 [4, 2048, 128], P('coil', 'rows')
All inputs are finite; a program needn't handle non-finite values. No bound on the sum of `sample_mask` on one device may be relied on, other than what follows from the above.
Results may differ from a plain program's by a relative error of at most 0.00011.
Values sent between devices are 32-bit elements; how exact they have to be, the bound alone decides.
A program may use at most 64 MiB of HBM per device.

v0:
```python
import jax
import jax.numpy as jnp
from jax import lax
from jax.sharding import PartitionSpec as P

KER = 64
ITERS = 2


threshold = 0.05


def shifted(block, axis, distance):
    devices = range(lax.axis_size(axis))
    route = [((i - distance) % len(devices), i) for i in devices]
    return lax.ppermute(block, axis, route)


def orthonormal(normal_rows, gram_matrix):
    factor = jnp.linalg.cholesky(gram_matrix)
    return lax.linalg.triangular_solve(
        factor, normal_rows, left_side=False, lower=True, transpose_a=True
    )


def coil_total(partial_value):
    return lax.psum(partial_value, "coil")


def shards(kspace, sample_mask, start_basis):
    highest = lax.Precision.HIGHEST
    channels = kspace.shape[0]
    tile_rows = kspace.shape[1]
    mask_float = sample_mask.astype(jnp.float32)
    sampled = kspace * mask_float
    next_rim = shifted(sampled[:, : KER - 1], "rows", -1)
    extended = jnp.concatenate([sampled, next_rim], axis=1)
    hankel_cols = jnp.stack(
        [extended[:, offset : offset + tile_rows] for offset in range(KER)], axis=0
    )
    hankel_cols = hankel_cols.reshape(KER * channels, tile_rows)
    owned_basis = start_basis.reshape(start_basis.shape[1], start_basis.shape[2])

    def fold_basis(shard_piece):
        return lax.dot_general(
            shard_piece,
            hankel_cols,
            (((0,), (0,)), ((), ())),
            precision=highest,
            preferred_element_type=jnp.float32,
        )

    def apply_hankel(current):
        partial_value = fold_basis(lax.all_gather(current, "rows", axis=0, tiled=True))
        return coil_total(partial_value)

    for iteration in range(ITERS):
        images = apply_hankel(owned_basis)
        normal_rows = lax.psum_scatter(
            lax.dot_general(
                hankel_cols,
                images,
                (((1,), (1,)), ((), ())),
                precision=highest,
                preferred_element_type=jnp.float32,
            ),
            "rows",
            scatter_dimension=0,
            tiled=True,
        )
        local_gram = jnp.dot(
            normal_rows.T, normal_rows, precision=highest, preferred_element_type=jnp.float32
        )
        gram_matrix = lax.psum(local_gram, ("rows", "coil"))
        owned_basis = orthonormal(normal_rows, gram_matrix)
    images = apply_hankel(owned_basis)
    projected = jnp.dot(
        lax.all_gather(owned_basis, "rows", axis=0, tiled=True),
        images,
        precision=highest,
        preferred_element_type=jnp.float32,
    )
    stacked = projected.reshape(KER, channels, tile_rows)
    spread = jnp.zeros((channels, tile_rows + KER - 1), jnp.float32)
    for offset in range(KER):
        spread = spread.at[:, offset : offset + tile_rows].add(stacked[offset])
    carried = shifted(spread[:, tile_rows:], "rows", 1)
    estimate = spread[:, :tile_rows].at[:, : KER - 1].add(carried) / KER
    residual = mask_float * (kspace - estimate)
    recovered = estimate + residual - jnp.clip(residual, -threshold, threshold)
    return (recovered, owned_basis.reshape(1, owned_basis.shape[0], owned_basis.shape[1]))


def solution(mesh):
    return jax.shard_map(
        shards,
        mesh=mesh,
        in_specs=(P("coil", "rows"), P("coil", "rows"), P("coil", "rows", None)),
        out_specs=(P("coil", "rows"), P("coil", "rows", None)),
        check_vma=False,
    )
```

profile of v0, /device:TPU:1, one launch (start us, length us, event | category | flops | bytes accessed | tf_op | source)
XLA Modules:
  0.0 1390.5 jit_solution(3663720347566413571)
XLA Ops:
  8.7 3.2 collective-permute-start
  57.3 34.4 %all-gather.9.cloned.1.call-done = f32[1,2048,128]{2,1,0:T(8,128)} async-done(((f32[1,32,128]{2,1,0:T(8,128)}), f32[1,2048,128]{2,1,0:T(8,128)}) %all-gather.9.cloned.1.call-update) | async-done | bytes 1048592 | tf_op jit(solution)/shard_map/all_gather | solution.py:54
  91.8 9.9 convolution_bitcast_fusion
  101.9 42.2 %all-reduce.7.cloned.1.call-done = f32[128,512]{0,1:T(8,128)} async-done(((f32[128,512]{0,1:T(8,128)}), f32[128,512]{0,1:T(8,128)}) %all-reduce.7.cloned.1.call-update) | async-done | bytes 262160 | tf_op jit(solution)/shard_map/psum | solution.py:27
  144.0 6.6 fusion.135
  150.7 137.7 %reduce-scatter.3.cloned.1.call-done = f32[32,128]{1,0:T(8,128)} async-done(((f32[2048,128]{1,0:T(8,128)}), f32[32,128]{1,0:T(8,128)}) %reduce-scatter.3.cloned.1.call-update) | async-done | bytes 16400 | tf_op jit(solution)/shard_map/reduce_scatter | solution.py:59
  288.5 1.7 fusion.136
  290.3 249.4 %all-reduce.9.cloned.1.call-done = f32[128,128]{0,1:T(8,128)} async-done(((f32[128,128]{0,1:T(8,128)}), f32[128,128]{0,1:T(8,128)}) %all-reduce.9.cloned.1.call-update) | async-done | bytes 65552 | tf_op jit(solution)/shard_map/psum | solution.py:74
  541.5 11.7 cholesky.44
  554.5 9.8 custom-call.6
  566.1 73.2 %all-gather.5.cloned.1.call-done = f32[2048,128]{1,0:T(8,128)} async-done(((f32[32,128]{1,0:T(8,128)}), f32[2048,128]{1,0:T(8,128)}) %all-gather.5.cloned.1.call-update) | async-done | bytes 1048592 | tf_op jit(solution)/shard_map/all_gather | solution.py:54
  639.3 5.8 fusion.137
  645.2 42.3 %all-reduce.11.cloned.1.call-done = f32[128,512]{1,0:T(8,128)} async-done(((f32[128,512]{1,0:T(8,128)}), f32[128,512]{1,0:T(8,128)}) %all-reduce.11.cloned.1.call-update) | async-done | bytes 262160 | tf_op jit(solution)/shard_map/psum | solution.py:27
  687.6 6.6 fusion.138
  694.3 137.8 %reduce-scatter.5.cloned.1.call-done = f32[32,128]{1,0:T(8,128)} async-done(((f32[2048,128]{1,0:T(8,128)}), f32[32,128]{1,0:T(8,128)}) %reduce-scatter.5.cloned.1.call-update) | async-done | bytes 16400 | tf_op jit(solution)/shard_map/reduce_scatter | solution.py:59
  832.0 1.7 fusion.139
  834.2 249.1 %all-reduce.13.cloned.1.call-done = f32[128,128]{0,1:T(8,128)} async-done(((f32[128,128]{0,1:T(8,128)}), f32[128,128]{0,1:T(8,128)}) %all-reduce.13.cloned.1.call-update) | async-done | bytes 65552 | tf_op jit(solution)/shard_map/psum | solution.py:74
  1085.2 11.7 cholesky.55
  1098.2 9.8 custom-call.7
  1109.6 73.4 %all-gather.7.cloned.1.call-done = f32[2048,128]{1,0:T(8,128)} async-done(((f32[32,128]{1,0:T(8,128)}), f32[2048,128]{1,0:T(8,128)}) %all-gather.7.cloned.1.call-update) | async-done | bytes 1048592 | tf_op jit(solution)/shard_map/all_gather | solution.py:78
  1183.0 5.9 fusion.140
  1231.5 4.5 fusion.141
  1251.9 1.6 add_select_fusion.54
  1256.4 1.6 add_select_fusion.52
  1278.9 1.6 add_select_fusion.42
  1281.2 1.6 add_select_fusion.41
  1294.7 1.6 add_select_fusion.35
  1301.5 1.6 add_select_fusion.32
  1308.2 1.6 add_select_fusion.29
  1321.7 1.6 add_select_fusion.23
  1371.1 1.6 add_select_fusion.1
  1376.6 3.8 collective-permute-start.1
  (296 shorter events, 227.9 us)
Async XLA Ops:
  7.2 84.6 %all-gather.9.cloned.1.call-start = ((), (), s32[]{:S(2)}) async-start(), calls=%async_computation.11 | async-start | bytes 1064960 | tf_op jit(solution)/shard_map/all_gather | solution.py:54
  8.7 4.0 collective-permute-start
  11.9 132.1 %all-reduce.7.cloned.1.call-start = ((), (), s32[]{:S(2)}) async-start(), calls=%async_computation.2 | async-start | bytes 524288 | tf_op jit(solution)/shard_map/psum | solution.py:27
  101.6 186.8 %reduce-scatter.3.cloned.1.call-start = ((), (), s32[]{:S(2)}) async-start(), calls=%async_computation.3 | async-start | bytes 1064960 | tf_op jit(solution)/shard_map/reduce_scatter | solution.py:59
  150.7 389.0 %all-reduce.9.cloned.1.call-start = ((), (), s32[]{:S(2)}) async-start(), calls=%async_computation.4 | async-start | bytes 131072 | tf_op jit(solution)/shard_map/psum | solution.py:74
  290.2 349.1 %all-gather.5.cloned.1.call-start = ((), (), s32[]{:S(2)}) async-start(), calls=%async_computation.5 | async-start | bytes 1064960 | tf_op jit(solution)/shard_map/all_gather | solution.py:54
  565.9 121.7 %all-reduce.11.cloned.1.call-start = ((), (), s32[]{:S(2)}) async-start(), calls=%async_computation.6 | async-start | bytes 524288 | tf_op jit(solution)/shard_map/psum | solution.py:27
  645.2 186.9 %reduce-scatter.5.cloned.1.call-start = ((), (), s32[]{:S(2)}) async-start(), calls=%async_computation.7 | async-start | bytes 1064960 | tf_op jit(solution)/shard_map/reduce_scatter | solution.py:59
  694.2 389.2 %all-reduce.13.cloned.1.call-start = ((), (), s32[]{:S(2)}) async-start(), calls=%async_computation.8 | async-start | bytes 131072 | tf_op jit(solution)/shard_map/psum | solution.py:74
  833.8 349.2 %all-gather.7.cloned.1.call-start = ((), (), s32[]{:S(2)}) async-start(), calls=%async_computation.9 | async-start | bytes 1064960 | tf_op jit(solution)/shard_map/all_gather | solution.py:78
  1109.6 121.9 %all-reduce.15.cloned.1.call-start = ((), (), s32[]{:S(2)}) async-start(), calls=%async_computation.10 | async-start | bytes 524288 | tf_op jit(solution)/shard_map/psum | solution.py:27
  1183.0 48.4 %copy-start.1 = (f32[2048,128]{1,0:T(8,128)S(1)}, f32[2048,128]{1,0:T(8,128)}, u32[]{:S(2)}) copy-start(f32[2048,128]{1,0:T(8,128)} %all-gather.7.cloned.1.call-done) | copy-start | bytes 3145732
  1235.9 2.0 copy-start
  1321.7 61.0 %copy-start.2 = (f32[32,512]{1,0:T(8,128)S(1)}, f32[32,512]{1,0:T(8,128)}, u32[]{:S(2)}) copy-start(f32[32,512]{1,0:T(8,128)} %param.136) | copy-start | bytes 196612
  1321.7 61.0 %copy-start.3 = (s32[32,512]{1,0:T(8,128)S(1)}, s32[32,512]{1,0:T(8,128)}, u32[]{:S(2)}) copy-start(s32[32,512]{1,0:T(8,128)} %param.137) | copy-start | bytes 196612
  1376.6 5.1 collective-permute-start.1
Sparse Core Ops, SparseCore 0:
  12.1 79.6 all-gather.8
  101.8 42.2 all-reduce.6
  150.8 137.6 reduce-scatter.2
  294.4 245.2 all-reduce.8
  566.0 73.3 all-gather.4
  645.3 42.2 all-reduce.10
  694.3 137.6 reduce-scatter.4
  838.1 245.1 all-reduce.12
  1109.7 73.3 all-gather.6
  1189.1 42.2 all-reduce.14
where the time goes:
time: 1400 us; the launch traced here: 1390 us
  waiting for transfers between devices  1040 us (74%)
  other arithmetic  234 us (17%)
  local copies, waits for them, and re-layouts  46 us (3%)
  matrix products  45.7 us (3%)
  between operations  15.6 us (1%)
    psum x2, waiting for transfers between devices, shards(): gram_matrix = lax.psum(local_gram, ('rows', 'coil'))  499 us
    reduce_scatter x2, waiting for transfers between devices, shards(): lax.psum_scatter(lax.dot_general(hankel_cols, images, (((1,), (1,)), ((),...  276 us
    another operation x128, other arithmetic  139 us
    all_gather x2, waiting for transfers between devices, apply_hankel(): lax.all_gather(current, 'rows', axis=0, tiled=True)  108 us
    psum x3, waiting for transfers between devices, coil_total(): return lax.psum(partial_value, 'coil')  84.5 us
    all_gather x1, waiting for transfers between devices, shards(): lax.all_gather(owned_basis, 'rows', axis=0, tiled=True)  73.4 us
    unnamed x63, other arithmetic  45.3 us
    scatter-add x64, local copies, waits for them, and re-layouts, shards(): spread = spread.at[:, offset:offset + tile_rows].add(stacked[offset])  43.2 us
  transfers between devices with their start and end apart: 12, of which 10 were waited for; matrix products, arithmetic and copies ran while one was open for 6% of the time, Pallas kernels for 0%

commit v1 on v0

v1 whole, which is shorter than its diff:
```python
import functools

import jax
import jax.numpy as jnp
from jax import lax
from jax.experimental import pallas as pl
from jax.experimental.pallas import tpu as pltpu
from jax.sharding import PartitionSpec as P

NZ, NX, NY = 8, 4, 4
ITERS = 2
CHG = 32
HALF = 512
RB = 16
THRESHOLD = 0.05
MESH = pl.DeviceIdType.MESH
HIGHEST = lax.Precision.HIGHEST
F32 = jnp.float32
BF16 = jnp.bfloat16
PAD = 128
SEMS = 176


def split(value):
    high = value.astype(BF16)
    return high, (value - high.astype(F32)).astype(BF16)


def mm(a, b, dims=((1,), (0,))):
    return lax.dot_general(a, b, (dims, ((), ())), preferred_element_type=F32)


def exact(a, b, dims=((1,), (0,))):
    return lax.dot_general(
        a, b, (dims, ((), ())), precision=HIGHEST, preferred_element_type=F32
    )


def near_first(n):
    return sorted(range(1, n), key=lambda k: min(k, n - k))


def kernel(
    ks_ref, mask_ref, basis_ref, rec_ref, bout_ref,
    own, sb, edge, halo, bt, vx, vo, vall, s3, s2t, ubuf, yh, yl,
    zp, rx, zs, rz, zo, pz, gz, gx, gp, aug, fac, vfull, ep, er, es, ey,
    send, recv,
):
    tiles = NZ * NX
    ch = NY * CHG
    width = 2 * HALF + 2 * PAD
    blocks = 2 * NY
    rank = blocks * RB
    rows = lax.axis_index("rows")
    y = lax.axis_index("coil")
    core = lax.rem(rows, 2)
    t = lax.div(rows, 2)
    x = lax.rem(t, NX)
    z = lax.div(t, NX)
    b = y * 2 + core
    used = [0]

    def dev(tile, c, yy):
        return (tile * 2 + c, yy)

    def slot():
        used[0] += 1
        return used[0] - 1

    def start(src, dst, device, i, j=None):
        copy = pltpu.make_async_remote_copy(
            src_ref=src, dst_ref=dst, send_sem=send.at[i],
            recv_sem=recv.at[i if j is None else j],
            device_id=device, device_id_type=MESH,
        )
        copy.start()
        return copy

    def arrived(dst, i):
        pltpu.make_async_remote_copy(
            src_ref=dst, dst_ref=dst, send_sem=send.at[i], recv_sem=recv.at[i],
            device_id=(rows, y), device_id_type=MESH,
        ).wait_recv()

    def at(zz, xx):
        return zz * NX + xx

    def plus(v, k, n):
        return lax.rem(v + k, n)

    ring = [(dy, dc) for dy in (0, 1, 3, 2) if dy < NY for dc in range(2)]
    peers = [p for p in ring if p != (0, 0)]
    before, after = plus(t, tiles - 1, tiles), plus(t, 1, tiles)

    barrier = pltpu.get_barrier_semaphore()
    greeted = 0
    for k in range(1, NZ):
        pl.semaphore_signal(barrier, inc=1, device_id=dev(at(plus(z, k, NZ), x), core, y), device_id_type=MESH)
        greeted += 1
    for k in range(1, NX):
        pl.semaphore_signal(barrier, inc=1, device_id=dev(at(z, plus(x, k, NX)), core, y), device_id_type=MESH)
        greeted += 1
    for dy, dc in peers:
        pl.semaphore_signal(barrier, inc=1, device_id=dev(t, plus(core, dc, 2), plus(y, dy, NY)), device_id_type=MESH)
        greeted += 1
    for tile in (before, after):
        for dy, dc in ring:
            pl.semaphore_signal(barrier, inc=1, device_id=dev(tile, plus(core, dc, 2), plus(y, dy, NY)), device_id_type=MESH)
            greeted += 1
    lanes = lax.broadcasted_iota(jnp.int32, (rank, ch), 1)
    tiled = jnp.concatenate([basis_ref[...]] * NY, axis=0).T
    placed = jnp.where(lax.div(lanes, CHG) == y, tiled, 0.0)
    bt[...] = placed.reshape(blocks, RB, ch)
    sampled = ks_ref[...] * mask_ref[...].astype(F32)
    own[...] = sampled
    edge[...] = jnp.where(core == 0, sampled[:, :PAD], sampled[:, HALF - PAD:])
    pl.semaphore_wait(barrier, greeted)

    waiting = []
    basis_in = []
    for dy, dc in peers:
        i = slot()
        yy, cc = plus(y, dy, NY), plus(core, dc, 2)
        waiting.append(start(bt.at[yy * 2 + cc], vx.at[core, y], dev(t, cc, yy), i))
        basis_in.append((plus(core, dc, 2), plus(y, NY - dy, NY), i))
    tile_in = []
    for dy, dc in peers:
        i = slot()
        yy, cc = plus(y, dy, NY), plus(core, dc, 2)
        waiting.append(start(own, sb.at[core, y], dev(t, cc, yy), i))
        tile_in.append((plus(core, dc, 2), plus(y, NY - dy, NY), i))
    halo_base = [slot() for _ in range(2 * NY)]
    target = lax.rem(t + tiles + 2 * core - 1, tiles)
    for dy, dc in ring:
        i = halo_base[dc * NY + dy]
        yy, cc = plus(y, dy, NY), plus(core, dc, 2)
        waiting.append(start(edge, halo.at[core, y], dev(target, cc, yy), i, halo_base[0] + core * NY + dy))
    vx[core, y] = bt[b]
    sb[core, y] = own[...]
    for cc, yy, i in basis_in:
        arrived(vx.at[cc, yy], i)
    for half in range(2):
        total = vx[half, 0]
        for yy in range(1, NY):
            total = total + vx[half, yy]
        vo[:, half * ch:(half + 1) * ch] = total

    def gather_basis():
        vall[t] = vo[...]
        sent = []
        order = near_first(NZ)
        first = {}
        for k in reversed(order):
            first[k] = slot()
            sent.append(start(vall.at[t], vall.at[t], dev(at(plus(z, k, NZ), x), core, y), first[k]))
        second = []
        for k in [0] + order:
            here = at(plus(z, NZ - k, NZ), x)
            if k:
                arrived(vall.at[here], first[k])
            for q in range(1, NX):
                i = slot()
                sent.append(start(vall.at[here], vall.at[here], dev(at(z, plus(x, q, NX)), core, y), i))
                second.append((at(plus(z, NZ - k, NZ), plus(x, NX - q, NX)), i))
        return sent, second

    def finish_gather(sent, second):
        for here, i in second:
            arrived(vall.at[here], i)
        for copy in sent:
            copy.wait_send()

    def analyse(store):
        for m in range(4):
            per = tiles // 4
            part = vall[m * per:(m + 1) * per].reshape(per * RB, 2 * ch)
            high, low = split(part)
            ubuf[m * per * RB:(m + 1) * per * RB, :] = mm(
                jnp.concatenate([high, high, low], axis=1), s3[...]
            )
        image = ubuf[0:RB, :]
        for i in range(1, tiles):
            image = image + pltpu.roll(ubuf[i * RB:(i + 1) * RB, :], width - 2 * i, 1)
        place = lax.broadcasted_iota(jnp.int32, (RB, width), 1)
        keep = place < PAD + 2 * HALF
        if store:
            keep = jnp.logical_and(keep, place >= PAD)
        image = jnp.where(keep, image, 0.0)
        for i in range(tiles):
            moved = image if i == 0 else pltpu.roll(image, 2 * i, 1)
            high, low = split(moved)
            yh[i * RB:(i + 1) * RB, :] = high
            yl[i * RB:(i + 1) * RB, :] = low

    def setup_tile():
        for cc, yy, i in tile_in:
            arrived(sb.at[cc, yy], i)
        for s in range(2):
            for dy in range(NY):
                arrived(halo.at[s, plus(y, NY - dy, NY)], halo_base[s * NY + dy])
        full = jnp.concatenate(
            [
                jnp.concatenate([halo[1, g], sb[0, g], sb[1, g], halo[0, g]], axis=1)
                for g in range(NY)
            ],
            axis=0,
        )
        pair = jnp.concatenate([full, pltpu.roll(full, width - 1, 1)], axis=0)
        high, low = split(pair)
        s3[0:2 * ch, :] = high
        s3[2 * ch:4 * ch, :] = low
        s3[4 * ch:6 * ch, :] = high
        turned_high, turned_low = split(pair.T)
        s2t[:, 0:2 * ch] = turned_high
        s2t[:, 2 * ch:4 * ch] = turned_low

    def normal_sum():
        per = tiles // 4
        for m in range(4):
            at_rows = slice(m * per * RB, (m + 1) * per * RB)
            high, low = yh[at_rows, :], yl[at_rows, :]
            main = s2t[:, 0:2 * ch]
            part = mm(high, main) + mm(low, main) + mm(high, s2t[:, 2 * ch:4 * ch])
            zp[m * per:(m + 1) * per] = part.reshape(per, RB, 2 * ch)
        sent = []
        order = near_first(NZ)[::-1] + [0]
        posts = []
        for o, k in enumerate(order):
            for q in range(1, NX):
                i = slot()
                xx = plus(x, q, NX)
                sent.append(start(zp.at[at(plus(z, k, NZ), xx)], rx.at[q - 1, o], dev(at(z, xx), core, y), i))
                posts.append(i)
        back = []
        for o, k in enumerate(order):
            for q in range(1, NX):
                arrived(rx.at[q - 1, o], posts[o * (NX - 1) + q - 1])
            total = zp[at(plus(z, k, NZ), x)]
            for q in range(1, NX):
                total = total + rx[q - 1, o]
            if k:
                zs[o] = total
                i = slot()
                sent.append(start(zs.at[o], rz.at[o], dev(at(plus(z, k, NZ), x), core, y), i))
                back.append((o, i))
            else:
                mine = total
        for o, i in back:
            arrived(rz.at[o], i)
            mine = mine + rz[o]
        zo[...] = mine
        return sent

    def exchange(src, ref_of, sent):
        posts = []
        for dy, dc in peers[::-1]:
            i = slot()
            yy, cc = plus(y, dy, NY), plus(core, dc, 2)
            sent.append(start(src, ref_of(b), dev(t, cc, yy), i))
            posts.append((plus(y, NY - dy, NY) * 2 + plus(core, dc, 2), i))
        for bb, i in posts[::-1]:
            arrived(ref_of(bb), i)

    def gram_sum(it, sent):
        pz[it, b] = zo[...]
        exchange(zo, lambda bb: pz.at[it, bb], sent)
        gathered = pz[it].reshape(rank, 2 * ch)
        gz[z] = exact(zo[...], gathered, ((1,), (1,)))
        posts = []
        for k in near_first(NZ)[::-1]:
            i = slot()
            sent.append(start(gz.at[z], gz.at[z], dev(at(plus(z, k, NZ), x), core, y), i))
            posts.append((plus(z, NZ - k, NZ), i))
        for zz, i in posts[::-1]:
            arrived(gz.at[zz], i)
        total = gz[0]
        for k in range(1, NZ):
            total = total + gz[k]
        gx[x] = total
        posts = []
        for k in near_first(NX)[::-1]:
            i = slot()
            sent.append(start(gx.at[x], gx.at[x], dev(at(z, plus(x, k, NX)), core, y), i))
            posts.append((plus(x, NX - k, NX), i))
        for xx, i in posts[::-1]:
            arrived(gx.at[xx], i)
        total = gx[0]
        for k in range(1, NX):
            total = total + gx[k]
        gp[b] = total
        exchange(gp.at[b], lambda bb: gp.at[bb], sent)
        return gathered

    def inverse_factor():
        line = lax.broadcasted_iota(jnp.int32, (rank, rank), 0)
        column = lax.broadcasted_iota(jnp.int32, (rank, rank), 1)
        aug[:, :rank] = gp[...].reshape(rank, rank)
        aug[:, rank:] = jnp.where(line == column, 1.0, 0.0).astype(F32)
        sub = lax.broadcasted_iota(jnp.int32, (8, rank), 0)

        def panel(k, carry):
            top = pl.multiple_of(k * 8, 8)
            left = aug[pl.ds(top, 8), :rank]
            right = aug[pl.ds(top, 8), rank:]
            turned = pltpu.roll(left, lax.rem(rank - k * 8, rank), 1)
            cols = [jnp.broadcast_to(turned[:, q:q + 1], (8, rank)) for q in range(8)]
            scale = jnp.zeros((8, rank), F32)
            for p in range(8):
                inverse_root = lax.rsqrt(jnp.broadcast_to(cols[p][p:p + 1, :], (8, rank)))
                step = jnp.where(sub > p, cols[p] * inverse_root * inverse_root, 0.0)
                scale = jnp.where(sub == p, inverse_root, scale)
                for q in range(p + 1, 8):
                    cols[q] = cols[q] - step * jnp.broadcast_to(cols[q][p:p + 1, :], (8, rank))
                left = left - step * jnp.broadcast_to(left[p:p + 1, :], (8, rank))
                right = right - step * jnp.broadcast_to(right[p:p + 1, :], (8, rank))
            both = jnp.concatenate([left * scale, right * scale], axis=1)
            fac[pl.ds(top, 8), :] = both[:, rank:]
            aug[...] = aug[...] - exact(both[:, :rank], both, ((0,), (0,)))
            return carry

        lax.fori_loop(0, rank // 8, panel, 0)

    def iteration(it, carry):
        sent, second = gather_basis()
        finish_gather(sent, second)
        analyse(True)
        sent = normal_sum()
        gathered = gram_sum(it, sent)
        inverse_factor()
        vfull[...] = exact(fac[...], gathered).reshape(blocks, RB, 2 * ch)
        for copy in sent:
            copy.wait_send()
        vo[...] = vfull[b]
        return carry

    setup_tile()
    lax.fori_loop(0, ITERS, iteration, 0)
    sent, second = gather_basis()
    finish_gather(sent, second)
    both = vfull[...].reshape(rank, 2 * ch)
    aug[:, :rank] = jnp.where(core == 0, both[:, :ch], both[:, ch:]).T
    bout_ref[...] = aug[pl.ds(pl.multiple_of(y * CHG, CHG), CHG), :rank]

    analyse(False)
    turned_high, turned_low = split(vall[...].reshape(tiles * RB, 2 * ch).T)
    for bit in range(2):
        at_rows = slice(bit * ch, (bit + 1) * ch)
        part = (
            mm(turned_high[at_rows], yh[...])
            + mm(turned_low[at_rows], yh[...])
            + mm(turned_high[at_rows], yl[...])
        )
        if bit:
            total = total + pltpu.roll(part, 1, 1)
        else:
            total = part
    for half in range(2):
        piece = total[:, PAD + half * HALF:PAD + (half + 1) * HALF]
        ep[half] = piece.reshape(NY, CHG, HALF)
    sent = []
    other = 1 - core
    order = near_first(NY)[::-1] + [0]
    posts = []
    for dy in order:
        i = slot()
        yy = plus(y, dy, NY)
        sent.append(start(ep.at[other, yy], er.at[yy], dev(t, other, y), i))
        posts.append(i)
    back = []
    for dy, i in zip(order, posts):
        yy = plus(y, dy, NY)
        arrived(er.at[yy], i)
        piece = ep[core, yy] + er[yy]
        if dy:
            es[dy] = piece
            j = slot()
            sent.append(start(es.at[dy], ey.at[dy], dev(t, core, yy), j))
            back.append((dy, j))
        else:
            estimate = piece
    for dy, j in back:
        arrived(ey.at[dy], j)
        estimate = estimate + ey[dy]
    estimate = estimate * (1.0 / (2 * tiles))
    residual = mask_ref[...].astype(F32) * (ks_ref[...] - estimate)
    rec_ref[...] = estimate + residual - jnp.clip(residual, -THRESHOLD, THRESHOLD)
    for copy in sent + waiting:
        copy.wait_send()
    assert used[0] <= SEMS, used[0]


def shards(kspace, sample_mask, start_basis):
    tiles = NZ * NX
    ch = NY * CHG
    width = 2 * HALF + 2 * PAD
    blocks = 2 * NY
    rank = blocks * RB
    vmem = pltpu.VMEM
    recovered, basis = pl.pallas_call(
        kernel,
        out_shape=(
            jax.ShapeDtypeStruct((CHG, HALF), F32),
            jax.ShapeDtypeStruct((CHG, rank), F32),
        ),
        in_specs=[pl.BlockSpec(memory_space=pltpu.VMEM)] * 3,
        out_specs=(pl.BlockSpec(memory_space=pltpu.VMEM),) * 2,
        scratch_shapes=[
            vmem((CHG, HALF), F32),
            vmem((2, NY, CHG, HALF), F32),
            vmem((CHG, PAD), F32),
            vmem((2, NY, CHG, PAD), F32),
            vmem((blocks, RB, ch), F32),
            vmem((2, NY, RB, ch), F32),
            vmem((RB, 2 * ch), F32),
            vmem((tiles, RB, 2 * ch), F32),
            vmem((6 * ch, width), BF16),
            vmem((width, 4 * ch), BF16),
            vmem((tiles * RB, width), F32),
            vmem((tiles * RB, width), BF16),
            vmem((tiles * RB, width), BF16),
            vmem((tiles, RB, 2 * ch), F32),
            vmem((max(NX - 1, 1), NZ, RB, 2 * ch), F32),
            vmem((NZ, RB, 2 * ch), F32),
            vmem((NZ, RB, 2 * ch), F32),
            vmem((RB, 2 * ch), F32),
            vmem((ITERS, blocks, RB, 2 * ch), F32),
            vmem((NZ, RB, rank), F32),
            vmem((NX, RB, rank), F32),
            vmem((blocks, RB, rank), F32),
            vmem((rank, 2 * rank), F32),
            vmem((rank, rank), F32),
            vmem((blocks, RB, 2 * ch), F32),
            vmem((2, NY, CHG, HALF), F32),
            vmem((NY, CHG, HALF), F32),
            vmem((NY, CHG, HALF), F32),
            vmem((NY, CHG, HALF), F32),
            pltpu.SemaphoreType.DMA((SEMS,)),
            pltpu.SemaphoreType.DMA((SEMS,)),
        ],
        compiler_params=pltpu.CompilerParams(
            collective_id=0, has_side_effects=True, vmem_limit_bytes=48 << 20
        ),
    )(kspace, sample_mask, start_basis.reshape(CHG, rank))
    return recovered, basis.reshape(1, CHG, rank)


def solution(mesh):
    return jax.shard_map(
        shards,
        mesh=mesh,
        in_specs=(P("coil", "rows"), P("coil", "rows"), P("coil", "rows", None)),
        out_specs=(P("coil", "rows"), P("coil", "rows", None)),
        check_vma=False,
    )
```

time: 1400 us -> 150 us (0.11)
  waiting for transfers between devices: 1040 us -> 0 us
  other arithmetic: 234 us -> 0 us
  Pallas kernels: 0 us -> 145 us
  matrix products: 45.7 us -> 0 us
  local copies, waits for them, and re-layouts: 46 us -> 3.63 us
  between operations: 15.6 us -> 0.65 us
    psum x5 -> x0, waiting for transfers between devices: 583 us -> none  [the longest x2 499 us: shards(): gram_matrix = lax.psum(local_gram, ('rows', 'coil'))]
    reduce_scatter x2 -> x0, waiting for transfers between devices: 276 us -> none  [shards(): lax.psum_scatter(lax.dot_general(hankel_cols, images, (((1,), (1,)), ((),...]
    another operation x139 -> x0, other arithmetic: 186 us -> none
    all_gather x3 -> x0, waiting for transfers between devices: 181 us -> none  [the longest x2 108 us: apply_hankel(): lax.all_gather(current, 'rows', axis=0, tiled=True)]
    pallas_call x0 -> x1, Pallas kernels: none -> 145 us  [shards(): pl.pallas_call(kernel, out_shape=(jax.ShapeDtypeStruct((CHG, HALF), F32),...]
    unnamed x63 -> x0, other arithmetic: 45.3 us -> none
    scatter-add x65 -> x0, local copies, waits for them, and re-layouts: 43.5 us -> none  [the longest x64 43.2 us: shards(): spread = spread.at[:, offset:offset + tile_rows].add(stacked[offset])]
    dot_general x8 -> x0, matrix products: 42.7 us -> none  [the longest x3 21.6 us: fold_basis(): lax.dot_general(shard_piece, hankel_cols, (((0,), (0,)), ((), ())), preci...]
  transfers between devices with their start and end apart: 12 -> 0, of which waited for: 10 -> 0; matrix products, arithmetic and copies ran while one was open for 6% -> 0% of each run, Pallas kernels for 0% -> 0%
where the time goes in v1:
time: 150 us
  Pallas kernels  145 us (97%)
  local copies, waits for them, and re-layouts  3.63 us (2%)
    pallas_call x1, Pallas kernels, shards(): pl.pallas_call(kernel, out_shape=(jax.ShapeDtypeStruct((CHG, HALF), F32),...  145 us
    unnamed x8, local copies, waits for them, and re-layouts  3.63 us

profile of v1, /device:TPU:1, one launch (start us, length us, event | category | flops | bytes accessed | tf_op | source)
XLA Modules:
  0.0 149.6 jit_solution(9428268301304686477)
XLA Ops:
  0.6 0.0 copy-start
  0.6 0.8 copy-done
  1.5 0.0 copy-start.1
  1.5 0.8 copy-done.1
  2.3 0.0 copy-start.2
  2.3 0.7 copy-done.2
  3.0 145.3 %shard_map.50 = (f32[32,512]{1,0:T(8,128)S(1)}, f32[32,128]{1,0:T(8,128)S(1)}) custom-call(f32[32,512]{1,0:T(8,128)S(1)} %copy-done, s32[32,512]{1,0:T(8,128)S(1)} %copy-done.1, f32[32,128]{1,0:T(8,128)S(1)} %bitcast.2), custom_call_target="tpu_custom_call" | custom-call | tf_op jit(solution)/shard_map/pallas_call | solution.py:399
  148.3 0.6 copy.7
  149.0 0.6 copy.8
Async XLA Ops:
  0.6 0.8 copy-start
  1.5 0.8 copy-start.1
  2.3 0.7 copy-start.2

commit v2 on v1

--- a/solution.py
+++ b/solution.py
@@ -18,7 +18,7 @@
 F32 = jnp.float32
 BF16 = jnp.bfloat16
 PAD = 128
-SEMS = 176
+SEMS = 256
 
 
 def split(value):
@@ -42,8 +42,8 @@
 
 def kernel(
     ks_ref, mask_ref, basis_ref, rec_ref, bout_ref,
-    own, sb, edge, halo, bt, vx, vo, vall, s3, s2t, ubuf, yh, yl,
-    zp, rx, zs, rz, zo, pz, gz, gx, gp, aug, fac, vfull, ep, er, es, ey,
+    own, sb, edge, halo, bt, vx, vall, s3, s2t, ubuf, yh, yl,
+    zp, rx, zs, rz, pz, gz, gx, gp, aug, fac, vfull, yx, ep, er, es, ey,
     send, recv,
 ):
     tiles = NZ * NX
@@ -139,41 +139,46 @@
     sb[core, y] = own[...]
     for cc, yy, i in basis_in:
         arrived(vx.at[cc, yy], i)
+    halves = []
     for half in range(2):
         total = vx[half, 0]
         for yy in range(1, NY):
             total = total + vx[half, yy]
-        vo[:, half * ch:(half + 1) * ch] = total
-
-    def gather_basis():
-        vall[t] = vo[...]
-        sent = []
-        order = near_first(NZ)
+        halves.append(total)
+    first_chunk = jnp.concatenate(halves, axis=1)
+
+    pending = []
+
+    def gather_start(it, chunk):
+        vall[it, t] = chunk
         first = {}
-        for k in reversed(order):
+        for k in near_first(NZ)[::-1]:
             first[k] = slot()
-            sent.append(start(vall.at[t], vall.at[t], dev(at(plus(z, k, NZ), x), core, y), first[k]))
+            pending.append(start(vall.at[it, t], vall.at[it, t], dev(at(plus(z, k, NZ), x), core, y), first[k]))
         second = []
-        for k in [0] + order:
-            here = at(plus(z, NZ - k, NZ), x)
+        gather_relay((it, first, second), (0,))
+        return it, first, second
+
+    def gather_relay(state, steps):
+        it, first, second = state
+        for k in steps:
+            zz = plus(z, NZ - k, NZ)
+            here = at(zz, x)
             if k:
-                arrived(vall.at[here], first[k])
+                arrived(vall.at[it, here], first[k])
             for q in range(1, NX):
                 i = slot()
-                sent.append(start(vall.at[here], vall.at[here], dev(at(z, plus(x, q, NX)), core, y), i))
-                second.append((at(plus(z, NZ - k, NZ), plus(x, NX - q, NX)), i))
-        return sent, second
-
-    def finish_gather(sent, second):
-        for here, i in second:
-            arrived(vall.at[here], i)
-        for copy in sent:
-            copy.wait_send()
-
-    def analyse(store):
+                pending.append(start(vall.at[it, here], vall.at[it, here], dev(at(z, plus(x, q, NX)), core, y), i))
+                second.append((at(zz, plus(x, NX - q, NX)), i))
+
+    def gather_finish(state):
+        for here, i in state[2]:
+            arrived(vall.at[state[0], here], i)
+
+    def analyse(it):
+        per = tiles // 4
         for m in range(4):
-            per = tiles // 4
-            part = vall[m * per:(m + 1) * per].reshape(per * RB, 2 * ch)
+            part = vall[it, m * per:(m + 1) * per].reshape(per * RB, 2 * ch)
             high, low = split(part)
             ubuf[m * per * RB:(m + 1) * per * RB, :] = mm(
                 jnp.concatenate([high, high, low], axis=1), s3[...]
@@ -181,11 +186,9 @@
         image = ubuf[0:RB, :]
         for i in range(1, tiles):
             image = image + pltpu.roll(ubuf[i * RB:(i + 1) * RB, :], width - 2 * i, 1)
-        place = lax.broadcasted_iota(jnp.int32, (RB, width), 1)
-        keep = place < PAD + 2 * HALF
-        if store:
-            keep = jnp.logical_and(keep, place >= PAD)
-        image = jnp.where(keep, image, 0.0)
+        return image
+
+    def spread(image):
         for i in range(tiles):
             moved = image if i == 0 else pltpu.roll(image, 2 * i, 1)
             high, low = split(moved)
@@ -214,88 +217,108 @@
         s2t[:, 0:2 * ch] = turned_high
         s2t[:, 2 * ch:4 * ch] = turned_low
 
-    def normal_sum():
+    far_first = near_first(NZ)[::-1] + [0]
+
+    def normal_start(it, image):
+        place = lax.broadcasted_iota(jnp.int32, (RB, width), 1)
+        spread(jnp.where(jnp.logical_and(place >= PAD, place < PAD + 2 * HALF), image, 0.0))
         per = tiles // 4
         for m in range(4):
             at_rows = slice(m * per * RB, (m + 1) * per * RB)
             high, low = yh[at_rows, :], yl[at_rows, :]
             main = s2t[:, 0:2 * ch]
             part = mm(high, main) + mm(low, main) + mm(high, s2t[:, 2 * ch:4 * ch])
-            zp[m * per:(m + 1) * per] = part.reshape(per, RB, 2 * ch)
-        sent = []
-        order = near_first(NZ)[::-1] + [0]
+            zp[it, m * per:(m + 1) * per] = part.reshape(per, RB, 2 * ch)
         posts = []
-        for o, k in enumerate(order):
+        for o, k in enumerate(far_first):
             for q in range(1, NX):
                 i = slot()
                 xx = plus(x, q, NX)
-                sent.append(start(zp.at[at(plus(z, k, NZ), xx)], rx.at[q - 1, o], dev(at(z, xx), core, y), i))
+                pending.append(start(zp.at[it, at(plus(z, k, NZ), xx)], rx.at[it, q - 1, o], dev(at(z, xx), core, y), i))
                 posts.append(i)
-        back = []
-        for o, k in enumerate(order):
-            for q in range(1, NX):
-                arrived(rx.at[q - 1, o], posts[o * (NX - 1) + q - 1])
-            total = zp[at(plus(z, k, NZ), x)]
-            for q in range(1, NX):
-                total = total + rx[q - 1, o]
-            if k:
-                zs[o] = total
-                i = slot()
-                sent.append(start(zs.at[o], rz.at[o], dev(at(plus(z, k, NZ), x), core, y), i))
-                back.append((o, i))
-            else:
-                mine = total
+        return it, posts, []
+
+    def normal_relay(state, o):
+        it, posts, back = state
+        k = far_first[o]
+        for q in range(1, NX):
+            arrived(rx.at[it, q - 1, o], posts[o * (NX - 1) + q - 1])
+        total = zp[it, at(plus(z, k, NZ), x)]
+        for q in range(1, NX):
+            total = total + rx[it, q - 1, o]
+        zs[it, o] = total
+        if k:
+            i = slot()
+            pending.append(start(zs.at[it, o], rz.at[it, o], dev(at(plus(z, k, NZ), x), core, y), i))
+            back.append((o, i))
+
+    def normal_finish(state):
+        it, _, back = state
+        mine = zs[it, NZ - 1]
         for o, i in back:
-            arrived(rz.at[o], i)
-            mine = mine + rz[o]
-        zo[...] = mine
-        return sent
-
-    def exchange(src, ref_of, sent):
+            arrived(rz.at[it, o], i)
+            mine = mine + rz[it, o]
+        return mine
+
+    def share(src, ref_of):
         posts = []
         for dy, dc in peers[::-1]:
             i = slot()
             yy, cc = plus(y, dy, NY), plus(core, dc, 2)
-            sent.append(start(src, ref_of(b), dev(t, cc, yy), i))
+            pending.append(start(src, ref_of(b), dev(t, cc, yy), i))
             posts.append((plus(y, NY - dy, NY) * 2 + plus(core, dc, 2), i))
+        return ref_of, posts
+
+    def shared(state):
+        ref_of, posts = state
         for bb, i in posts[::-1]:
             arrived(ref_of(bb), i)
 
-    def gram_sum(it, sent):
-        pz[it, b] = zo[...]
-        exchange(zo, lambda bb: pz.at[it, bb], sent)
-        gathered = pz[it].reshape(rank, 2 * ch)
-        gz[z] = exact(zo[...], gathered, ((1,), (1,)))
+    def rows_share(it, chunk):
+        pz[it, b] = chunk
+        return share(pz.at[it, b], lambda bb: pz.at[it, bb])
+
+    def along_z(it, product):
+        gz[it, z] = product
         posts = []
         for k in near_first(NZ)[::-1]:
             i = slot()
-            sent.append(start(gz.at[z], gz.at[z], dev(at(plus(z, k, NZ), x), core, y), i))
+            pending.append(start(gz.at[it, z], gz.at[it, z], dev(at(plus(z, k, NZ), x), core, y), i))
             posts.append((plus(z, NZ - k, NZ), i))
+        return it, posts
+
+    def along_x(state):
+        it, posts = state
         for zz, i in posts[::-1]:
-            arrived(gz.at[zz], i)
-        total = gz[0]
+            arrived(gz.at[it, zz], i)
+        total = gz[it, 0]
         for k in range(1, NZ):
-            total = total + gz[k]
-        gx[x] = total
+            total = total + gz[it, k]
+        gx[it, x] = total
         posts = []
         for k in near_first(NX)[::-1]:
             i = slot()
-            sent.append(start(gx.at[x], gx.at[x], dev(at(z, plus(x, k, NX)), core, y), i))
+            pending.append(start(gx.at[it, x], gx.at[it, x], dev(at(z, plus(x, k, NX)), core, y), i))
             posts.append((plus(x, NX - k, NX), i))
+        return it, posts
+
+    def gram_share(state):
+        it, posts = state
         for xx, i in posts[::-1]:
-            arrived(gx.at[xx], i)
-        total = gx[0]
+            arrived(gx.at[it, xx], i)
+        total = gx[it, 0]
         for k in range(1, NX):
-            total = total + gx[k]
-        gp[b] = total
-        exchange(gp.at[b], lambda bb: gp.at[bb], sent)
-        return gathered
-
-    def inverse_factor():
+            total = total + gx[it, k]
+        gp[it, b] = total
+        return share(gp.at[it, b], lambda bb: gp.at[it, bb])
+
+    def factor_start(it):
         line = lax.broadcasted_iota(jnp.int32, (rank, rank), 0)
         column = lax.broadcasted_iota(jnp.int32, (rank, rank), 1)
-        aug[:, :rank] = gp[...].reshape(rank, rank)
+        aug[:, :rank] = gp[it].reshape(rank, rank)
         aug[:, rank:] = jnp.where(line == column, 1.0, 0.0).astype(F32)
+
+    def factor_panels(it, low, high):
         sub = lax.broadcasted_iota(jnp.int32, (8, rank), 0)
 
         def panel(k, carry):
@@ -314,35 +337,71 @@
                 left = left - step * jnp.broadcast_to(left[p:p + 1, :], (8, rank))
                 right = right - step * jnp.broadcast_to(right[p:p + 1, :], (8, rank))
             both = jnp.concatenate([left * scale, right * scale], axis=1)
-            fac[pl.ds(top, 8), :] = both[:, rank:]
+            fac[it, pl.ds(top, 8), :] = both[:, rank:]
             aug[...] = aug[...] - exact(both[:, :rank], both, ((0,), (0,)))
             return carry
 
-        lax.fori_loop(0, rank // 8, panel, 0)
-
-    def iteration(it, carry):
-        sent, second = gather_basis()
-        finish_gather(sent, second)
-        analyse(True)
-        sent = normal_sum()
-        gathered = gram_sum(it, sent)
-        inverse_factor()
-        vfull[...] = exact(fac[...], gathered).reshape(blocks, RB, 2 * ch)
-        for copy in sent:
-            copy.wait_send()
-        vo[...] = vfull[b]
-        return carry
-
+        lax.fori_loop(low, high, panel, 0)
+
+    panels = rank // 8
+    order = near_first(NZ)
+    moving = gather_start(0, first_chunk)
     setup_tile()
-    lax.fori_loop(0, ITERS, iteration, 0)
-    sent, second = gather_basis()
-    finish_gather(sent, second)
-    both = vfull[...].reshape(rank, 2 * ch)
+    gather_relay(moving, order)
+    gather_finish(moving)
+    folding = normal_start(0, analyse(0))
+    for o in range(NZ):
+        normal_relay(folding, o)
+    chunk = normal_finish(folding)
+
+    moving = gather_start(1, chunk)
+    joined = rows_share(0, chunk)
+    gather_relay(moving, order)
+    shared(joined)
+    gram = along_z(0, exact(pz[0, b], pz[0].reshape(rank, 2 * ch), ((1,), (1,))))
+    gather_finish(moving)
+    image = analyse(1)
+    gram = along_x(gram)
+    folding = normal_start(1, image)
+    gram = gram_share(gram)
+    head = max(NZ - 5, 1)
+    for o in range(head):
+        normal_relay(folding, o)
+    shared(gram)
+    factor_start(0)
+    for o in range(head, NZ):
+        at_panel = 2 * (o - head)
+        factor_panels(0, at_panel, at_panel + 2)
+        normal_relay(folding, o)
+    factor_panels(0, 2 * (NZ - head), panels)
+    chunk = normal_finish(folding)
+    joined = rows_share(1, chunk)
+    shared(joined)
+    vfull[...] = exact(fac[0], pz[1].reshape(rank, 2 * ch)).reshape(blocks, RB, 2 * ch)
+
+    chunk = vfull[b]
+    gram = along_z(1, exact(chunk, vfull[...].reshape(rank, 2 * ch), ((1,), (1,))))
+    moving = gather_start(2, chunk)
+    gather_relay(moving, order[:4])
+    gram = along_x(gram)
+    gather_relay(moving, order[4:])
+    gram = gram_share(gram)
+    gather_finish(moving)
+    yx[b] = analyse(2)[:, :width - PAD]
+    joined = share(yx.at[b], lambda bb: yx.at[bb])
+    turned_high, turned_low = split(vall[2].reshape(tiles * RB, 2 * ch).T)
+    shared(gram)
+    factor_start(1)
+    factor_panels(1, 0, panels)
+    inverse = fac[1]
+    fac[0] = inverse.T
+    both = exact(inverse, vfull[...].reshape(rank, 2 * ch))
     aug[:, :rank] = jnp.where(core == 0, both[:, :ch], both[:, ch:]).T
     bout_ref[...] = aug[pl.ds(pl.multiple_of(y * CHG, CHG), CHG), :rank]
-
-    analyse(False)
-    turned_high, turned_low = split(vall[...].reshape(tiles * RB, 2 * ch).T)
+    weights = exact(fac[0, pl.ds(pl.multiple_of(b * RB, RB), RB), :], inverse)
+    shared(joined)
+    image = exact(weights, yx[...].reshape(rank, width - PAD))
+    spread(jnp.concatenate([image, jnp.zeros((RB, PAD), F32)], axis=1))
     for bit in range(2):
         at_rows = slice(bit * ch, (bit + 1) * ch)
         part = (
@@ -357,14 +416,13 @@
     for half in range(2):
         piece = total[:, PAD + half * HALF:PAD + (half + 1) * HALF]
         ep[half] = piece.reshape(NY, CHG, HALF)
-    sent = []
     other = 1 - core
     order = near_first(NY)[::-1] + [0]
     posts = []
     for dy in order:
         i = slot()
         yy = plus(y, dy, NY)
-        sent.append(start(ep.at[other, yy], er.at[yy], dev(t, other, y), i))
+        pending.append(start(ep.at[other, yy], er.at[yy], dev(t, other, y), i))
         posts.append(i)
     back = []
     for dy, i in zip(order, posts):
@@ -374,7 +432,7 @@
         if dy:
             es[dy] = piece
             j = slot()
-            sent.append(start(es.at[dy], ey.at[dy], dev(t, core, yy), j))
+            pending.append(start(es.at[dy], ey.at[dy], dev(t, core, yy), j))
             back.append((dy, j))
         else:
             estimate = piece
@@ -384,7 +442,7 @@
     estimate = estimate * (1.0 / (2 * tiles))
     residual = mask_ref[...].astype(F32) * (ks_ref[...] - estimate)
     rec_ref[...] = estimate + residual - jnp.clip(residual, -THRESHOLD, THRESHOLD)
-    for copy in sent + waiting:
+    for copy in pending + waiting:
         copy.wait_send()
     assert used[0] <= SEMS, used[0]
 
@@ -411,25 +469,24 @@
             vmem((2, NY, CHG, PAD), F32),
             vmem((blocks, RB, ch), F32),
             vmem((2, NY, RB, ch), F32),
-            vmem((RB, 2 * ch), F32),
-            vmem((tiles, RB, 2 * ch), F32),
+            vmem((ITERS + 1, tiles, RB, 2 * ch), F32),
             vmem((6 * ch, width), BF16),
             vmem((width, 4 * ch), BF16),
             vmem((tiles * RB, width), F32),
             vmem((tiles * RB, width), BF16),
             vmem((tiles * RB, width), BF16),
-            vmem((tiles, RB, 2 * ch), F32),
-            vmem((max(NX - 1, 1), NZ, RB, 2 * ch), F32),
-            vmem((NZ, RB, 2 * ch), F32),
-            vmem((NZ, RB, 2 * ch), F32),
-            vmem((RB, 2 * ch), F32),
+            vmem((ITERS, tiles, RB, 2 * ch), F32),
+            vmem((ITERS, max(NX - 1, 1), NZ, RB, 2 * ch), F32),
+            vmem((ITERS, NZ, RB, 2 * ch), F32),
+            vmem((ITERS, NZ, RB, 2 * ch), F32),
             vmem((ITERS, blocks, RB, 2 * ch), F32),
-            vmem((NZ, RB, rank), F32),
-            vmem((NX, RB, rank), F32),
-            vmem((blocks, RB, rank), F32),
+            vmem((ITERS, NZ, RB, rank), F32),
+            vmem((ITERS, NX, RB, rank), F32),
+            vmem((ITERS, blocks, RB, rank), F32),
             vmem((rank, 2 * rank), F32),
-            vmem((rank, rank), F32),
+            vmem((ITERS, rank, rank), F32),
             vmem((blocks, RB, 2 * ch), F32),
+            vmem((blocks, RB, width - PAD), F32),
             vmem((2, NY, CHG, HALF), F32),
             vmem((NY, CHG, HALF), F32),
             vmem((NY, CHG, HALF), F32),

time: 150 us -> 118 us (0.79)
  Pallas kernels: 145 us -> 114 us
    pallas_call x1, Pallas kernels: 145 us -> 114 us  [shards(): pl.pallas_call(kernel, out_shape=(jax.ShapeDtypeStruct((CHG, HALF), F32),...]
where the time goes in v2:
time: 118 us
  Pallas kernels  114 us (97%)
  local copies, waits for them, and re-layouts  3.63 us (3%)
    pallas_call x1, Pallas kernels, shards(): pl.pallas_call(kernel, out_shape=(jax.ShapeDtypeStruct((CHG, HALF), F32),...  114 us
    unnamed x8, local copies, waits for them, and re-layouts  3.63 us

profile of v2, /device:TPU:1, one launch (start us, length us, event | category | flops | bytes accessed | tf_op | source)
XLA Modules:
  0.0 118.3 jit_solution(16807404119890434251)
XLA Ops:
  0.6 0.0 copy-start
  0.6 0.8 copy-done
  1.5 0.0 copy-start.1
  1.5 0.8 copy-done.1
  2.3 0.0 copy-start.2
  2.3 0.7 copy-done.2
  3.0 114.0 %shard_map.50 = (f32[32,512]{1,0:T(8,128)S(1)}, f32[32,128]{1,0:T(8,128)S(1)}) custom-call(f32[32,512]{1,0:T(8,128)S(1)} %copy-done, s32[32,512]{1,0:T(8,128)S(1)} %copy-done.1, f32[32,128]{1,0:T(8,128)S(1)} %bitcast.2), custom_call_target="tpu_custom_call" | custom-call | tf_op jit(solution)/shard_map/pallas_call | solution.py:457
  117.0 0.6 copy.7
  117.6 0.6 copy.8
Async XLA Ops:
  0.6 0.8 copy-start
  1.5 0.8 copy-start.1
  2.3 0.7 copy-start.2

commit v3 on v2

--- a/solution.py
+++ b/solution.py
@@ -18,6 +18,7 @@
 F32 = jnp.float32
 BF16 = jnp.bfloat16
 PAD = 128
+PANEL = 16
 SEMS = 256
 
 
@@ -41,11 +42,19 @@
 
 
 def kernel(
-    ks_ref, mask_ref, basis_ref, rec_ref, bout_ref,
-    own, sb, edge, halo, bt, vx, vall, s3, s2t, ubuf, yh, yl,
+    ks_hbm, mask_hbm, basis_hbm, rec_ref, bout_ref,
+    ks_ref, mask_ref, basis_ref, own, sb, edge, halo, bt, vx, vall, s3, s2t, ubuf, yh, yl,
     zp, rx, zs, rz, pz, gz, gx, gp, aug, fac, vfull, yx, ep, er, es, ey,
-    send, recv,
+    send, recv, load,
 ):
+    loads = [
+        pltpu.make_async_copy(src, dst, load.at[i])
+        for i, (src, dst) in enumerate(
+            ((basis_hbm, basis_ref), (ks_hbm, ks_ref), (mask_hbm, mask_ref))
+        )
+    ]
+    for copy in loads:
+        copy.start()
     tiles = NZ * NX
     ch = NY * CHG
     width = 2 * HALF + 2 * PAD
@@ -107,6 +116,8 @@
         for dy, dc in ring:
             pl.semaphore_signal(barrier, inc=1, device_id=dev(tile, plus(core, dc, 2), plus(y, dy, NY)), device_id_type=MESH)
             greeted += 1
+    for copy in loads:
+        copy.wait()
     lanes = lax.broadcasted_iota(jnp.int32, (rank, ch), 1)
     tiled = jnp.concatenate([basis_ref[...]] * NY, axis=0).T
     placed = jnp.where(lax.div(lanes, CHG) == y, tiled, 0.0)
@@ -152,7 +163,7 @@
     def gather_start(it, chunk):
         vall[it, t] = chunk
         first = {}
-        for k in near_first(NZ)[::-1]:
+        for k in near_first(NZ):
             first[k] = slot()
             pending.append(start(vall.at[it, t], vall.at[it, t], dev(at(plus(z, k, NZ), x), core, y), first[k]))
         second = []
@@ -171,8 +182,8 @@
                 pending.append(start(vall.at[it, here], vall.at[it, here], dev(at(z, plus(x, q, NX)), core, y), i))
                 second.append((at(zz, plus(x, NX - q, NX)), i))
 
-    def gather_finish(state):
-        for here, i in state[2]:
+    def gather_finish(state, low=0, high=None):
+        for here, i in state[2][low:high]:
             arrived(vall.at[state[0], here], i)
 
     def analyse(it):
@@ -319,35 +330,43 @@
         aug[:, rank:] = jnp.where(line == column, 1.0, 0.0).astype(F32)
 
     def factor_panels(it, low, high):
-        sub = lax.broadcasted_iota(jnp.int32, (8, rank), 0)
+        sub = lax.broadcasted_iota(jnp.int32, (PANEL, rank), 0)
 
         def panel(k, carry):
-            top = pl.multiple_of(k * 8, 8)
-            left = aug[pl.ds(top, 8), :rank]
-            right = aug[pl.ds(top, 8), rank:]
-            turned = pltpu.roll(left, lax.rem(rank - k * 8, rank), 1)
-            cols = [jnp.broadcast_to(turned[:, q:q + 1], (8, rank)) for q in range(8)]
-            scale = jnp.zeros((8, rank), F32)
-            for p in range(8):
-                inverse_root = lax.rsqrt(jnp.broadcast_to(cols[p][p:p + 1, :], (8, rank)))
-                step = jnp.where(sub > p, cols[p] * inverse_root * inverse_root, 0.0)
-                scale = jnp.where(sub == p, inverse_root, scale)
-                for q in range(p + 1, 8):
-                    cols[q] = cols[q] - step * jnp.broadcast_to(cols[q][p:p + 1, :], (8, rank))
-                left = left - step * jnp.broadcast_to(left[p:p + 1, :], (8, rank))
-                right = right - step * jnp.broadcast_to(right[p:p + 1, :], (8, rank))
-            both = jnp.concatenate([left * scale, right * scale], axis=1)
-            fac[it, pl.ds(top, 8), :] = both[:, rank:]
-            aug[...] = aug[...] - exact(both[:, :rank], both, ((0,), (0,)))
+            top = pl.multiple_of(k * PANEL, PANEL)
+            left = aug[pl.ds(top, PANEL), :rank]
+            right = aug[pl.ds(top, PANEL), rank:]
+            turned = pltpu.roll(left, lax.rem(rank - k * PANEL, rank), 1)
+            cols = [jnp.broadcast_to(turned[:, q:q + 1], (PANEL, rank)) for q in range(PANEL)]
+            done_left = jnp.zeros((PANEL, rank), F32)
+            done_right = done_left
+
+            def line(value, p):
+                return jnp.broadcast_to(value[p:p + 1, :], (PANEL, rank))
+
+            for p in range(PANEL):
+                root = lax.rsqrt(line(cols[p], p))
+                step = cols[p] * root
+                for q in range(p + 1, PANEL):
+                    cols[q] = cols[q] - step * (line(cols[q], p) * root)
+                left_line = line(left, p) * root
+                right_line = line(right, p) * root
+                done_left = jnp.where(sub == p, left_line, done_left)
+                done_right = jnp.where(sub == p, right_line, done_right)
+                left = left - step * left_line
+                right = right - step * right_line
+            both = jnp.concatenate([done_left, done_right], axis=1)
+            fac[it, pl.ds(top, PANEL), :] = done_right
+            aug[...] = aug[...] - exact(done_left, both, ((0,), (0,)))
             return carry
 
         lax.fori_loop(low, high, panel, 0)
 
-    panels = rank // 8
+    panels = rank // PANEL
     order = near_first(NZ)
     moving = gather_start(0, first_chunk)
+    gather_relay(moving, order)
     setup_tile()
-    gather_relay(moving, order)
     gather_finish(moving)
     folding = normal_start(0, analyse(0))
     for o in range(NZ):
@@ -356,12 +375,15 @@
 
     moving = gather_start(1, chunk)
     joined = rows_share(0, chunk)
-    gather_relay(moving, order)
+    gather_relay(moving, order[:2])
     shared(joined)
     gram = along_z(0, exact(pz[0, b], pz[0].reshape(rank, 2 * ch), ((1,), (1,))))
-    gather_finish(moving)
+    gather_relay(moving, order[2:])
+    early = (NX - 1) * (NZ // 2)
+    gather_finish(moving, 0, early)
+    gram = along_x(gram)
+    gather_finish(moving, early)
     image = analyse(1)
-    gram = along_x(gram)
     folding = normal_start(1, image)
     gram = gram_share(gram)
     head = max(NZ - 5, 1)
@@ -370,10 +392,9 @@
     shared(gram)
     factor_start(0)
     for o in range(head, NZ):
-        at_panel = 2 * (o - head)
-        factor_panels(0, at_panel, at_panel + 2)
+        factor_panels(0, o - head, o - head + 1)
         normal_relay(folding, o)
-    factor_panels(0, 2 * (NZ - head), panels)
+    factor_panels(0, NZ - head, panels)
     chunk = normal_finish(folding)
     joined = rows_share(1, chunk)
     shared(joined)
@@ -460,9 +481,12 @@
             jax.ShapeDtypeStruct((CHG, HALF), F32),
             jax.ShapeDtypeStruct((CHG, rank), F32),
         ),
-        in_specs=[pl.BlockSpec(memory_space=pltpu.VMEM)] * 3,
+        in_specs=[pl.BlockSpec(memory_space=pl.ANY)] * 3,
         out_specs=(pl.BlockSpec(memory_space=pltpu.VMEM),) * 2,
         scratch_shapes=[
+            vmem((CHG, HALF), F32),
+            vmem((CHG, HALF), jnp.int32),
+            vmem((CHG, rank), F32),
             vmem((CHG, HALF), F32),
             vmem((2, NY, CHG, HALF), F32),
             vmem((CHG, PAD), F32),
@@ -493,6 +517,7 @@
             vmem((NY, CHG, HALF), F32),
             pltpu.SemaphoreType.DMA((SEMS,)),
             pltpu.SemaphoreType.DMA((SEMS,)),
+            pltpu.SemaphoreType.DMA((3,)),
         ],
         compiler_params=pltpu.CompilerParams(
             collective_id=0, has_side_effects=True, vmem_limit_bytes=48 << 20

time: 118 us -> 107 us (0.907)
  Pallas kernels: 114 us -> 102 us
    pallas_call x1, Pallas kernels: 114 us -> 102 us  [shards(): pl.pallas_call(kernel, out_shape=(jax.ShapeDtypeStruct((CHG, HALF), F32),...]
where the time goes in v3:
time: 107 us
  Pallas kernels  102 us (95%)
  local copies, waits for them, and re-layouts  3.63 us (3%)
    pallas_call x1, Pallas kernels, shards(): pl.pallas_call(kernel, out_shape=(jax.ShapeDtypeStruct((CHG, HALF), F32),...  102 us
    unnamed x8, local copies, waits for them, and re-layouts  3.63 us

profile of v3, /device:TPU:1, one launch (start us, length us, event | category | flops | bytes accessed | tf_op | source)
XLA Modules:
  0.0 106.7 jit_solution(774593708053967184)
XLA Ops:
  0.6 0.0 copy-start
  0.6 0.8 copy-done
  1.5 0.0 copy-start.1
  1.5 0.8 copy-done.1
  2.3 0.0 copy-start.2
  2.3 0.7 copy-done.2
  3.0 102.4 %shard_map.50 = (f32[32,512]{1,0:T(8,128)S(1)}, f32[32,128]{1,0:T(8,128)S(1)}) custom-call(f32[32,512]{1,0:T(8,128)S(1)} %copy-done, s32[32,512]{1,0:T(8,128)S(1)} %copy-done.1, f32[32,128]{1,0:T(8,128)S(1)} %bitcast.2), custom_call_target="tpu_custom_call" | custom-call | tf_op jit(solution)/shard_map/pallas_call | solution.py:478
  105.4 0.6 copy.7
  106.1 0.6 copy.8
Async XLA Ops:
  0.6 0.8 copy-start
  1.5 0.8 copy-start.1
  2.3 0.7 copy-start.2

commit v4 on v3

--- a/solution.py
+++ b/solution.py
@@ -182,18 +182,23 @@
                 pending.append(start(vall.at[it, here], vall.at[it, here], dev(at(z, plus(x, q, NX)), core, y), i))
                 second.append((at(zz, plus(x, NX - q, NX)), i))
 
-    def gather_finish(state, low=0, high=None):
-        for here, i in state[2][low:high]:
-            arrived(vall.at[state[0], here], i)
-
-    def analyse(it):
-        per = tiles // 4
-        for m in range(4):
-            part = vall[it, m * per:(m + 1) * per].reshape(per * RB, 2 * ch)
-            high, low = split(part)
-            ubuf[m * per * RB:(m + 1) * per * RB, :] = mm(
-                jnp.concatenate([high, high, low], axis=1), s3[...]
-            )
+    def gather_multiply(state, pairs):
+        it, _, second = state
+        slabs = [0] + near_first(NZ)
+        for u in pairs:
+            for here, i in second[2 * u * (NX - 1):2 * (u + 1) * (NX - 1)]:
+                arrived(vall.at[it, here], i)
+            parts, places = [], []
+            for k in slabs[2 * u:2 * u + 2]:
+                zz = plus(z, NZ - k, NZ)
+                parts.append(vall[it, pl.ds(zz * NX, NX)].reshape(NX * RB, 2 * ch))
+                places.append(pl.multiple_of(zz * NX * RB, NX * RB))
+            high, low = split(jnp.concatenate(parts, axis=0))
+            product = mm(jnp.concatenate([high, high, low], axis=1), s3[...])
+            for w, place in enumerate(places):
+                ubuf[pl.ds(place, NX * RB), :] = product[w * NX * RB:(w + 1) * NX * RB]
+
+    def analyse():
         image = ubuf[0:RB, :]
         for i in range(1, tiles):
             image = image + pltpu.roll(ubuf[i * RB:(i + 1) * RB, :], width - 2 * i, 1)
@@ -228,47 +233,56 @@
         s2t[:, 0:2 * ch] = turned_high
         s2t[:, 2 * ch:4 * ch] = turned_low
 
-    far_first = near_first(NZ)[::-1] + [0]
-
-    def normal_start(it, image):
+    couples = NZ // 2
+    far_first = near_first(couples)[::-1] + [0]
+
+    def normal_start(it, image, hook=None):
         place = lax.broadcasted_iota(jnp.int32, (RB, width), 1)
         spread(jnp.where(jnp.logical_and(place >= PAD, place < PAD + 2 * HALF), image, 0.0))
-        per = tiles // 4
-        for m in range(4):
-            at_rows = slice(m * per * RB, (m + 1) * per * RB)
+        half, odd = lax.div(z, 2), lax.rem(z, 2)
+        steps = []
+        for g in far_first:
+            pair = plus(half, g, couples)
+            size = 2 * NX * RB
+            at_rows = pl.ds(pl.multiple_of(pair * size, size), size)
             high, low = yh[at_rows, :], yl[at_rows, :]
             main = s2t[:, 0:2 * ch]
             part = mm(high, main) + mm(low, main) + mm(high, s2t[:, 2 * ch:4 * ch])
-            zp[it, m * per:(m + 1) * per] = part.reshape(per, RB, 2 * ch)
-        posts = []
-        for o, k in enumerate(far_first):
-            for q in range(1, NX):
-                i = slot()
-                xx = plus(x, q, NX)
-                pending.append(start(zp.at[it, at(plus(z, k, NZ), xx)], rx.at[it, q - 1, o], dev(at(z, xx), core, y), i))
-                posts.append(i)
-        return it, posts, []
+            zp[it, pl.ds(pair * 2 * NX, 2 * NX)] = part.reshape(2 * NX, RB, 2 * ch)
+            for w in range(2):
+                o = len(steps)
+                zz = 2 * pair + w if g else 2 * half + (odd if w else 1 - odd)
+                posts = []
+                for q in range(1, NX):
+                    i = slot()
+                    xx = plus(x, q, NX)
+                    pending.append(start(zp.at[it, at(zz, xx)], rx.at[it, q - 1, o], dev(at(z, xx), core, y), i))
+                    posts.append(i)
+                steps.append((zz, posts))
+            if hook is not None and len(steps) == min(4, NZ):
+                hook()
+        return it, steps, [slot() for _ in range(NZ)]
 
     def normal_relay(state, o):
-        it, posts, back = state
-        k = far_first[o]
+        it, steps, back = state
+        zz, posts = steps[o]
         for q in range(1, NX):
-            arrived(rx.at[it, q - 1, o], posts[o * (NX - 1) + q - 1])
-        total = zp[it, at(plus(z, k, NZ), x)]
+            arrived(rx.at[it, q - 1, o], posts[q - 1])
+        total = zp[it, at(zz, x)]
         for q in range(1, NX):
             total = total + rx[it, q - 1, o]
         zs[it, o] = total
-        if k:
-            i = slot()
-            pending.append(start(zs.at[it, o], rz.at[it, o], dev(at(plus(z, k, NZ), x), core, y), i))
-            back.append((o, i))
+        if o < NZ - 1:
+            away = lax.rem(zz - z + NZ, NZ)
+            pending.append(start(zs.at[it, o], rz.at[it, z], dev(at(zz, x), core, y), back[o], back[0] + away))
 
     def normal_finish(state):
         it, _, back = state
         mine = zs[it, NZ - 1]
-        for o, i in back:
-            arrived(rz.at[it, o], i)
-            mine = mine + rz[it, o]
+        for k in range(1, NZ):
+            source = plus(z, NZ - k, NZ)
+            arrived(rz.at[it, source], back[0] + k)
+            mine = mine + rz[it, source]
         return mine
 
     def share(src, ref_of):
@@ -367,8 +381,9 @@
     moving = gather_start(0, first_chunk)
     gather_relay(moving, order)
     setup_tile()
-    gather_finish(moving)
-    folding = normal_start(0, analyse(0))
+    every = range(couples)
+    gather_multiply(moving, every)
+    folding = normal_start(0, analyse())
     for o in range(NZ):
         normal_relay(folding, o)
     chunk = normal_finish(folding)
@@ -379,13 +394,12 @@
     shared(joined)
     gram = along_z(0, exact(pz[0, b], pz[0].reshape(rank, 2 * ch), ((1,), (1,))))
     gather_relay(moving, order[2:])
-    early = (NX - 1) * (NZ // 2)
-    gather_finish(moving, 0, early)
+    gather_multiply(moving, every[:couples // 2])
     gram = along_x(gram)
-    gather_finish(moving, early)
-    image = analyse(1)
-    folding = normal_start(1, image)
-    gram = gram_share(gram)
+    gather_multiply(moving, every[couples // 2:])
+    grams = []
+    folding = normal_start(1, analyse(), lambda: grams.append(gram_share(gram)))
+    gram = grams[0]
     head = max(NZ - 5, 1)
     for o in range(head):
         normal_relay(folding, o)
@@ -407,8 +421,8 @@
     gram = along_x(gram)
     gather_relay(moving, order[4:])
     gram = gram_share(gram)
-    gather_finish(moving)
-    yx[b] = analyse(2)[:, :width - PAD]
+    gather_multiply(moving, every)
+    yx[b] = analyse()[:, :width - PAD]
     joined = share(yx.at[b], lambda bb: yx.at[bb])
     turned_high, turned_low = split(vall[2].reshape(tiles * RB, 2 * ch).T)
     shared(gram)
@@ -416,9 +430,6 @@
     factor_panels(1, 0, panels)
     inverse = fac[1]
     fac[0] = inverse.T
-    both = exact(inverse, vfull[...].reshape(rank, 2 * ch))
-    aug[:, :rank] = jnp.where(core == 0, both[:, :ch], both[:, ch:]).T
-    bout_ref[...] = aug[pl.ds(pl.multiple_of(y * CHG, CHG), CHG), :rank]
     weights = exact(fac[0, pl.ds(pl.multiple_of(b * RB, RB), RB), :], inverse)
     shared(joined)
     image = exact(weights, yx[...].reshape(rank, width - PAD))
@@ -457,6 +468,9 @@
             back.append((dy, j))
         else:
             estimate = piece
+    both = exact(inverse, vfull[...].reshape(rank, 2 * ch))
+    aug[:, :rank] = jnp.where(core == 0, both[:, :ch], both[:, ch:]).T
+    bout_ref[...] = aug[pl.ds(pl.multiple_of(y * CHG, CHG), CHG), :rank]
     for dy, j in back:
         arrived(ey.at[dy], j)
         estimate = estimate + ey[dy]
@@ -481,7 +495,7 @@
             jax.ShapeDtypeStruct((CHG, HALF), F32),
             jax.ShapeDtypeStruct((CHG, rank), F32),
         ),
-        in_specs=[pl.BlockSpec(memory_space=pl.ANY)] * 3,
+        in_specs=[pl.BlockSpec(memory_space=pltpu.HBM)] * 3,
         out_specs=(pl.BlockSpec(memory_space=pltpu.VMEM),) * 2,
         scratch_shapes=[
             vmem((CHG, HALF), F32),
@@ -520,7 +534,7 @@
             pltpu.SemaphoreType.DMA((3,)),
         ],
         compiler_params=pltpu.CompilerParams(
-            collective_id=0, has_side_effects=True, vmem_limit_bytes=48 << 20
+            collective_id=0, has_side_effects=True, vmem_limit_bytes=67043328
         ),
     )(kspace, sample_mask, start_basis.reshape(CHG, rank))
     return recovered, basis.reshape(1, CHG, rank)

time: 107 us -> 106 us (level)
  local copies, waits for them, and re-layouts: 3.63 us -> 2.09 us
    unnamed x8 -> x4, local copies, waits for them, and re-layouts: 3.63 us -> 2.09 us
where the time goes in v4:
time: 106 us; the launch traced here: 105 us
  Pallas kernels  103 us (97%)
  local copies, waits for them, and re-layouts  2.09 us (2%)
    pallas_call x1, Pallas kernels, shards(): pl.pallas_call(kernel, out_shape=(jax.ShapeDtypeStruct((CHG, HALF), F32),...  103 us

profile of v4, /device:TPU:1, one launch (start us, length us, event | category | flops | bytes accessed | tf_op | source)
XLA Modules:
  0.0 105.4 jit_solution(10375600433101489387)
XLA Ops:
  0.6 102.6 %shard_map.50 = (f32[32,512]{1,0:T(8,128)}, f32[32,128]{1,0:T(8,128)}) custom-call(f32[32,512]{1,0:T(8,128)} %ks_hbm.1, s32[32,512]{1,0:T(8,128)} %mask_hbm.1, f32[32,128]{1,0:T(8,128)} %bitcast.2), custom_call_target="tpu_custom_call" | custom-call | tf_op jit(solution)/shard_map/pallas_call | solution.py:492
  103.3 0.0 copy-start
  103.3 1.5 %copy.7 = f32[32,512]{1,0:T(8,128)} copy(f32[32,512]{1,0:T(8,128)} %get-tuple-element.8) | data formatting | bytes 131072
  104.8 0.0 copy-done
  104.8 0.6 copy.8
Async XLA Ops:
  103.3 1.5 %copy-start = (f32[32,128]{1,0:T(8,128)S(1)}, f32[32,128]{1,0:T(8,128)}, u32[]{:S(2)}) copy-start(f32[32,128]{1,0:T(8,128)} %get-tuple-element.5) | copy-start | bytes 49156

commit v5 on v3

--- a/solution.py
+++ b/solution.py
@@ -43,8 +43,8 @@
 
 def kernel(
     ks_hbm, mask_hbm, basis_hbm, rec_ref, bout_ref,
-    ks_ref, mask_ref, basis_ref, own, sb, edge, halo, bt, vx, vall, s3, s2t, ubuf, yh, yl,
-    zp, rx, zs, rz, pz, gz, gx, gp, aug, fac, vfull, yx, ep, er, es, ey,
+    ks_ref, mask_ref, basis_ref, own, sb, edge, halo, bt, vx, vall, s8h, s8l, s8th, s8tl, turned, yh, yl,
+    zp, rx, zs, rz, pz, gz, gx, gp, aug, fac, vfull, ys, yx, es, ey,
     send, recv, load,
 ):
     loads = [
@@ -58,6 +58,7 @@
     tiles = NZ * NX
     ch = NY * CHG
     width = 2 * HALF + 2 * PAD
+    span = HALF + PAD
     blocks = 2 * NY
     rank = blocks * RB
     rows = lax.axis_index("rows")
@@ -187,24 +188,16 @@
             arrived(vall.at[state[0], here], i)
 
     def analyse(it):
-        per = tiles // 4
-        for m in range(4):
-            part = vall[it, m * per:(m + 1) * per].reshape(per * RB, 2 * ch)
-            high, low = split(part)
-            ubuf[m * per * RB:(m + 1) * per * RB, :] = mm(
-                jnp.concatenate([high, high, low], axis=1), s3[...]
-            )
-        image = ubuf[0:RB, :]
-        for i in range(1, tiles):
-            image = image + pltpu.roll(ubuf[i * RB:(i + 1) * RB, :], width - 2 * i, 1)
+        slabs = vall[it].reshape(NZ, NX, RB, 2 * ch)
+        joined = jnp.concatenate(
+            [slabs[:, q].reshape(NZ * RB, 2 * ch) for q in range(NX)], axis=1
+        )
+        high, low = split(joined)
+        product = mm(high, s8h[...]) + mm(high, s8l[...]) + mm(low, s8h[...])
+        image = product[0:RB]
+        for k in range(1, NZ):
+            image = image + pltpu.roll(product[k * RB:(k + 1) * RB], width - 2 * NX * k, 1)
         return image
-
-    def spread(image):
-        for i in range(tiles):
-            moved = image if i == 0 else pltpu.roll(image, 2 * i, 1)
-            high, low = split(moved)
-            yh[i * RB:(i + 1) * RB, :] = high
-            yl[i * RB:(i + 1) * RB, :] = low
 
     def setup_tile():
         for cc, yy, i in tile_in:
@@ -219,56 +212,60 @@
             ],
             axis=0,
         )
-        pair = jnp.concatenate([full, pltpu.roll(full, width - 1, 1)], axis=0)
-        high, low = split(pair)
-        s3[0:2 * ch, :] = high
-        s3[2 * ch:4 * ch, :] = low
-        s3[4 * ch:6 * ch, :] = high
-        turned_high, turned_low = split(pair.T)
-        s2t[:, 0:2 * ch] = turned_high
-        s2t[:, 2 * ch:4 * ch] = turned_low
+        for shift in range(2 * NX):
+            moved = full if shift == 0 else pltpu.roll(full, width - shift, 1)
+            high, low = split(moved)
+            s8h[shift * ch:(shift + 1) * ch, :] = high
+            s8l[shift * ch:(shift + 1) * ch, :] = low
+        turned[0:width, :] = full.T
+        turned[width:width + 8, :] = jnp.zeros((8, ch), F32)
+        for shift in range(2 * NX):
+            high, low = split(turned[shift:shift + width, :])
+            s8th[:, shift * ch:(shift + 1) * ch] = high
+            s8tl[:, shift * ch:(shift + 1) * ch] = low
 
     far_first = near_first(NZ)[::-1] + [0]
 
-    def normal_start(it, image):
+    def normal_start(it, image, hook=None):
         place = lax.broadcasted_iota(jnp.int32, (RB, width), 1)
-        spread(jnp.where(jnp.logical_and(place >= PAD, place < PAD + 2 * HALF), image, 0.0))
-        per = tiles // 4
-        for m in range(4):
-            at_rows = slice(m * per * RB, (m + 1) * per * RB)
-            high, low = yh[at_rows, :], yl[at_rows, :]
-            main = s2t[:, 0:2 * ch]
-            part = mm(high, main) + mm(low, main) + mm(high, s2t[:, 2 * ch:4 * ch])
-            zp[it, m * per:(m + 1) * per] = part.reshape(per, RB, 2 * ch)
-        posts = []
-        for o, k in enumerate(far_first):
-            for q in range(1, NX):
+        image = jnp.where(jnp.logical_and(place >= PAD, place < PAD + 2 * HALF), image, 0.0)
+        moved = [image] + [pltpu.roll(image, 2 * NX * k, 1) for k in range(1, NZ)]
+        high, low = split(jnp.concatenate(moved, axis=0))
+        posts = {}
+        for q in near_first(NX)[::-1] + [0]:
+            if q == 0 and hook is not None:
+                hook()
+            xx = plus(x, q, NX)
+            lanes_at = pl.ds(pl.multiple_of(xx * 2 * ch, 2 * ch), 2 * ch)
+            main = s8th[:, lanes_at]
+            part = mm(high, main) + mm(low, main) + mm(high, s8tl[:, lanes_at])
+            zp[it, xx] = part.reshape(NZ, RB, 2 * ch)
+            for o, k in enumerate(far_first if q else ()):
                 i = slot()
-                xx = plus(x, q, NX)
-                pending.append(start(zp.at[it, at(plus(z, k, NZ), xx)], rx.at[it, q - 1, o], dev(at(z, xx), core, y), i))
-                posts.append(i)
-        return it, posts, []
+                pending.append(start(zp.at[it, xx, plus(z, k, NZ)], rx.at[it, q - 1, o], dev(at(z, xx), core, y), i))
+                posts[q, o] = i
+        return it, posts, [slot() for _ in range(NZ)]
 
     def normal_relay(state, o):
         it, posts, back = state
-        k = far_first[o]
+        zz = plus(z, far_first[o], NZ)
         for q in range(1, NX):
-            arrived(rx.at[it, q - 1, o], posts[o * (NX - 1) + q - 1])
-        total = zp[it, at(plus(z, k, NZ), x)]
+            arrived(rx.at[it, q - 1, o], posts[q, o])
+        total = zp[it, x, zz]
         for q in range(1, NX):
             total = total + rx[it, q - 1, o]
         zs[it, o] = total
-        if k:
-            i = slot()
-            pending.append(start(zs.at[it, o], rz.at[it, o], dev(at(plus(z, k, NZ), x), core, y), i))
-            back.append((o, i))
+        if far_first[o]:
+            i = back[far_first[o]]
+            pending.append(start(zs.at[it, o], rz.at[it, z], dev(at(zz, x), core, y), i))
 
     def normal_finish(state):
         it, _, back = state
         mine = zs[it, NZ - 1]
-        for o, i in back:
-            arrived(rz.at[it, o], i)
-            mine = mine + rz[it, o]
+        for k in range(1, NZ):
+            source = plus(z, NZ - k, NZ)
+            arrived(rz.at[it, source], back[k])
+            mine = mine + rz[it, source]
         return mine
 
     def share(src, ref_of):
@@ -383,9 +380,9 @@
     gather_finish(moving, 0, early)
     gram = along_x(gram)
     gather_finish(moving, early)
-    image = analyse(1)
-    folding = normal_start(1, image)
-    gram = gram_share(gram)
+    grams = []
+    folding = normal_start(1, analyse(1), lambda: grams.append(gram_share(gram)))
+    gram = grams[0]
     head = max(NZ - 5, 1)
     for o in range(head):
         normal_relay(folding, o)
@@ -402,27 +399,41 @@
 
     chunk = vfull[b]
     gram = along_z(1, exact(chunk, vfull[...].reshape(rank, 2 * ch), ((1,), (1,))))
-    moving = gather_start(2, chunk)
+    moving = gather_start(2 + core, chunk)
     gather_relay(moving, order[:4])
     gram = along_x(gram)
     gather_relay(moving, order[4:])
     gram = gram_share(gram)
     gather_finish(moving)
-    yx[b] = analyse(2)[:, :width - PAD]
-    joined = share(yx.at[b], lambda bb: yx.at[bb])
-    turned_high, turned_low = split(vall[2].reshape(tiles * RB, 2 * ch).T)
+    other = 1 - core
+    swap = slot()
+    pending.append(start(vall.at[2 + core], vall.at[2 + core], dev(t, other, y), swap))
+    image = analyse(2 + core)
+    for half in range(2):
+        ys[half] = image[:, half * HALF:half * HALF + span]
+    yx[b] = ys[core]
+    posts = []
+    for dy, dc in peers[::-1]:
+        i = slot()
+        yy, cc = plus(y, dy, NY), plus(core, dc, 2)
+        pending.append(start(ys.at[cc], yx.at[b], dev(t, cc, yy), i))
+        posts.append((plus(y, NY - dy, NY) * 2 + plus(core, dc, 2), i))
+    joined = (lambda bb: yx.at[bb]), posts
+    arrived(vall.at[2 + other], swap)
+    both_blocks = jnp.concatenate([vall[2], vall[3]], axis=1).reshape(tiles * 2 * RB, 2 * ch)
+    turned_high, turned_low = split(both_blocks.T)
     shared(gram)
     factor_start(1)
     factor_panels(1, 0, panels)
     inverse = fac[1]
     fac[0] = inverse.T
-    both = exact(inverse, vfull[...].reshape(rank, 2 * ch))
-    aug[:, :rank] = jnp.where(core == 0, both[:, :ch], both[:, ch:]).T
-    bout_ref[...] = aug[pl.ds(pl.multiple_of(y * CHG, CHG), CHG), :rank]
-    weights = exact(fac[0, pl.ds(pl.multiple_of(b * RB, RB), RB), :], inverse)
+    weights = exact(fac[0, pl.ds(pl.multiple_of(y * 2 * RB, 2 * RB), 2 * RB), :], inverse)
     shared(joined)
-    image = exact(weights, yx[...].reshape(rank, width - PAD))
-    spread(jnp.concatenate([image, jnp.zeros((RB, PAD), F32)], axis=1))
+    image = exact(weights, yx[...].reshape(rank, span))
+    for i in range(tiles):
+        high, low = split(image if i == 0 else pltpu.roll(image, 2 * i, 1))
+        yh[i * 2 * RB:(i + 1) * 2 * RB, :] = high
+        yl[i * 2 * RB:(i + 1) * 2 * RB, :] = low
     for bit in range(2):
         at_rows = slice(bit * ch, (bit + 1) * ch)
         part = (
@@ -434,29 +445,17 @@
             total = total + pltpu.roll(part, 1, 1)
         else:
             total = part
-    for half in range(2):
-        piece = total[:, PAD + half * HALF:PAD + (half + 1) * HALF]
-        ep[half] = piece.reshape(NY, CHG, HALF)
-    other = 1 - core
-    order = near_first(NY)[::-1] + [0]
-    posts = []
-    for dy in order:
-        i = slot()
+    es[...] = total[:, PAD:].reshape(NY, CHG, HALF)
+    back = []
+    for dy in near_first(NY)[::-1]:
+        j = slot()
         yy = plus(y, dy, NY)
-        pending.append(start(ep.at[other, yy], er.at[yy], dev(t, other, y), i))
-        posts.append(i)
-    back = []
-    for dy, i in zip(order, posts):
-        yy = plus(y, dy, NY)
-        arrived(er.at[yy], i)
-        piece = ep[core, yy] + er[yy]
-        if dy:
-            es[dy] = piece
-            j = slot()
-            pending.append(start(es.at[dy], ey.at[dy], dev(t, core, yy), j))
-            back.append((dy, j))
-        else:
-            estimate = piece
+        pending.append(start(es.at[yy], ey.at[dy], dev(t, core, yy), j))
+        back.append((dy, j))
+    estimate = es[y]
+    both = exact(inverse, vfull[...].reshape(rank, 2 * ch))
+    aug[:, :rank] = jnp.where(core == 0, both[:, :ch], both[:, ch:]).T
+    bout_ref[...] = aug[pl.ds(pl.multiple_of(y * CHG, CHG), CHG), :rank]
     for dy, j in back:
         arrived(ey.at[dy], j)
         estimate = estimate + ey[dy]
@@ -472,6 +471,7 @@
     tiles = NZ * NX
     ch = NY * CHG
     width = 2 * HALF + 2 * PAD
+    span = HALF + PAD
     blocks = 2 * NY
     rank = blocks * RB
     vmem = pltpu.VMEM
@@ -481,7 +481,7 @@
             jax.ShapeDtypeStruct((CHG, HALF), F32),
             jax.ShapeDtypeStruct((CHG, rank), F32),
         ),
-        in_specs=[pl.BlockSpec(memory_space=pl.ANY)] * 3,
+        in_specs=[pl.BlockSpec(memory_space=pltpu.HBM)] * 3,
         out_specs=(pl.BlockSpec(memory_space=pltpu.VMEM),) * 2,
         scratch_shapes=[
             vmem((CHG, HALF), F32),
@@ -493,13 +493,15 @@
             vmem((2, NY, CHG, PAD), F32),
             vmem((blocks, RB, ch), F32),
             vmem((2, NY, RB, ch), F32),
-            vmem((ITERS + 1, tiles, RB, 2 * ch), F32),
-            vmem((6 * ch, width), BF16),
-            vmem((width, 4 * ch), BF16),
-            vmem((tiles * RB, width), F32),
-            vmem((tiles * RB, width), BF16),
-            vmem((tiles * RB, width), BF16),
-            vmem((ITERS, tiles, RB, 2 * ch), F32),
+            vmem((ITERS + 2, tiles, RB, 2 * ch), F32),
+            vmem((2 * NX * ch, width), BF16),
+            vmem((2 * NX * ch, width), BF16),
+            vmem((width, 2 * NX * ch), BF16),
+            vmem((width, 2 * NX * ch), BF16),
+            vmem((width + 8, ch), F32),
+            vmem((tiles * 2 * RB, span), BF16),
+            vmem((tiles * 2 * RB, span), BF16),
+            vmem((ITERS, NX, NZ, RB, 2 * ch), F32),
             vmem((ITERS, max(NX - 1, 1), NZ, RB, 2 * ch), F32),
             vmem((ITERS, NZ, RB, 2 * ch), F32),
             vmem((ITERS, NZ, RB, 2 * ch), F32),
@@ -510,9 +512,8 @@
             vmem((rank, 2 * rank), F32),
             vmem((ITERS, rank, rank), F32),
             vmem((blocks, RB, 2 * ch), F32),
-            vmem((blocks, RB, width - PAD), F32),
-            vmem((2, NY, CHG, HALF), F32),
-            vmem((NY, CHG, HALF), F32),
+            vmem((2, RB, span), F32),
+            vmem((blocks, RB, span), F32),
             vmem((NY, CHG, HALF), F32),
             vmem((NY, CHG, HALF), F32),
             pltpu.SemaphoreType.DMA((SEMS,)),
@@ -520,7 +521,7 @@
             pltpu.SemaphoreType.DMA((3,)),
         ],
         compiler_params=pltpu.CompilerParams(
-            collective_id=0, has_side_effects=True, vmem_limit_bytes=48 << 20
+            collective_id=0, has_side_effects=True, vmem_limit_bytes=67043328
         ),
     )(kspace, sample_mask, start_basis.reshape(CHG, rank))
     return recovered, basis.reshape(1, CHG, rank)

time: 107 us -> 105 us (0.981)
  local copies, waits for them, and re-layouts: 3.63 us -> 2.09 us
    unnamed x8 -> x4, local copies, waits for them, and re-layouts: 3.63 us -> 2.09 us
where the time goes in v5:
time: 105 us
  Pallas kernels  102 us (97%)
  local copies, waits for them, and re-layouts  2.09 us (2%)
    pallas_call x1, Pallas kernels, shards(): pl.pallas_call(kernel, out_shape=(jax.ShapeDtypeStruct((CHG, HALF), F32),...  102 us

profile of v5, /device:TPU:1, one launch (start us, length us, event | category | flops | bytes accessed | tf_op | source)
XLA Modules:
  0.0 104.6 jit_solution(6734951164599137007)
XLA Ops:
  0.6 101.8 %shard_map.50 = (f32[32,512]{1,0:T(8,128)}, f32[32,128]{1,0:T(8,128)}) custom-call(f32[32,512]{1,0:T(8,128)} %ks_hbm.1, s32[32,512]{1,0:T(8,128)} %mask_hbm.1, f32[32,128]{1,0:T(8,128)} %bitcast.2), custom_call_target="tpu_custom_call" | custom-call | tf_op jit(solution)/shard_map/pallas_call | solution.py:478
  102.5 0.0 copy-start
  102.5 1.5 %copy.7 = f32[32,512]{1,0:T(8,128)} copy(f32[32,512]{1,0:T(8,128)} %get-tuple-element.8) | data formatting | bytes 131072
  104.0 0.0 copy-done
  104.0 0.6 copy.8
Async XLA Ops:
  102.5 1.5 %copy-start = (f32[32,128]{1,0:T(8,128)S(1)}, f32[32,128]{1,0:T(8,128)}, u32[]{:S(2)}) copy-start(f32[32,128]{1,0:T(8,128)} %get-tuple-element.5) | copy-start | bytes 49156

commit v6 on v5

--- a/solution.py
+++ b/solution.py
@@ -193,7 +193,9 @@
             [slabs[:, q].reshape(NZ * RB, 2 * ch) for q in range(NX)], axis=1
         )
         high, low = split(joined)
-        product = mm(high, s8h[...]) + mm(high, s8l[...]) + mm(low, s8h[...])
+        size = NZ * RB
+        main = mm(jnp.concatenate([high, low], axis=0), s8h[...])
+        product = main[:size] + main[size:] + mm(high, s8l[...])
         image = product[0:RB]
         for k in range(1, NZ):
             image = image + pltpu.roll(product[k * RB:(k + 1) * RB], width - 2 * NX * k, 1)
@@ -231,14 +233,16 @@
         image = jnp.where(jnp.logical_and(place >= PAD, place < PAD + 2 * HALF), image, 0.0)
         moved = [image] + [pltpu.roll(image, 2 * NX * k, 1) for k in range(1, NZ)]
         high, low = split(jnp.concatenate(moved, axis=0))
+        stacked = jnp.concatenate([high, low], axis=0)
+        size = NZ * RB
         posts = {}
         for q in near_first(NX)[::-1] + [0]:
             if q == 0 and hook is not None:
                 hook()
             xx = plus(x, q, NX)
             lanes_at = pl.ds(pl.multiple_of(xx * 2 * ch, 2 * ch), 2 * ch)
-            main = s8th[:, lanes_at]
-            part = mm(high, main) + mm(low, main) + mm(high, s8tl[:, lanes_at])
+            main = mm(stacked, s8th[:, lanes_at])
+            part = main[:size] + main[size:] + mm(high, s8tl[:, lanes_at])
             zp[it, xx] = part.reshape(NZ, RB, 2 * ch)
             for o, k in enumerate(far_first if q else ()):
                 i = slot()
@@ -434,17 +438,9 @@
         high, low = split(image if i == 0 else pltpu.roll(image, 2 * i, 1))
         yh[i * 2 * RB:(i + 1) * 2 * RB, :] = high
         yl[i * 2 * RB:(i + 1) * 2 * RB, :] = low
-    for bit in range(2):
-        at_rows = slice(bit * ch, (bit + 1) * ch)
-        part = (
-            mm(turned_high[at_rows], yh[...])
-            + mm(turned_low[at_rows], yh[...])
-            + mm(turned_high[at_rows], yl[...])
-        )
-        if bit:
-            total = total + pltpu.roll(part, 1, 1)
-        else:
-            total = part
+    main = mm(jnp.concatenate([turned_high, turned_low], axis=0), yh[...])
+    part = main[:2 * ch] + main[2 * ch:] + mm(turned_high, yl[...])
+    total = part[:ch] + pltpu.roll(part[ch:], 1, 1)
     es[...] = total[:, PAD:].reshape(NY, CHG, HALF)
     back = []
     for dy in near_first(NY)[::-1]:
@@ -456,13 +452,15 @@
     both = exact(inverse, vfull[...].reshape(rank, 2 * ch))
     aug[:, :rank] = jnp.where(core == 0, both[:, :ch], both[:, ch:]).T
     bout_ref[...] = aug[pl.ds(pl.multiple_of(y * CHG, CHG), CHG), :rank]
+    for copy in waiting + pending[:-(NY - 1)]:
+        copy.wait_send()
     for dy, j in back:
         arrived(ey.at[dy], j)
         estimate = estimate + ey[dy]
     estimate = estimate * (1.0 / (2 * tiles))
     residual = mask_ref[...].astype(F32) * (ks_ref[...] - estimate)
     rec_ref[...] = estimate + residual - jnp.clip(residual, -THRESHOLD, THRESHOLD)
-    for copy in pending + waiting:
+    for copy in pending[-(NY - 1):]:
         copy.wait_send()
     assert used[0] <= SEMS, used[0]
 
@@ -475,6 +473,7 @@
     blocks = 2 * NY
     rank = blocks * RB
     vmem = pltpu.VMEM
+    operands = (kspace, sample_mask, start_basis.reshape(CHG, rank))
     recovered, basis = pl.pallas_call(
         kernel,
         out_shape=(
@@ -521,9 +520,9 @@
             pltpu.SemaphoreType.DMA((3,)),
         ],
         compiler_params=pltpu.CompilerParams(
-            collective_id=0, has_side_effects=True, vmem_limit_bytes=67043328
+            collective_id=0, has_side_effects=True, vmem_limit_bytes=48 << 20
         ),
-    )(kspace, sample_mask, start_basis.reshape(CHG, rank))
+    )(*[pltpu.with_memory_space_constraint(v, pltpu.HBM) for v in operands])
     return recovered, basis.reshape(1, CHG, rank)
 
 

time: 105 us -> 102 us (0.971)
  Pallas kernels: 102 us -> 100 us
    pallas_call x1, Pallas kernels: 102 us -> 100 us  [shards(): pl.pallas_call(kernel, out_shape=(jax.ShapeDtypeStruct((CHG, HALF), F32),...]
where the time goes in v6:
time: 102 us
  Pallas kernels  100 us (98%)
  local copies, waits for them, and re-layouts  1.24 us (1%)
    pallas_call x1, Pallas kernels, shards(): pl.pallas_call(kernel, out_shape=(jax.ShapeDtypeStruct((CHG, HALF), F32),...  100 us

profile of v6, /device:TPU:1, one launch (start us, length us, event | category | flops | bytes accessed | tf_op | source)
XLA Modules:
  0.0 102.2 jit_solution(16082891945172531804)
XLA Ops:
  0.6 100.3 %shard_map.50 = (f32[32,512]{1,0:T(8,128)S(1)}, f32[32,128]{1,0:T(8,128)S(1)}) custom-call(f32[32,512]{1,0:T(8,128)} %ks_hbm.1, s32[32,512]{1,0:T(8,128)} %mask_hbm.1, f32[32,128]{1,0:T(8,128)} %bitcast.3), custom_call_target="tpu_custom_call" | custom-call | tf_op jit(solution)/shard_map/pallas_call | solution.py:477
  100.9 0.6 copy.7
  101.6 0.6 copy.8

commit v7 on v6

--- a/solution.py
+++ b/solution.py
@@ -187,19 +187,41 @@
         for here, i in state[2][low:high]:
             arrived(vall.at[state[0], here], i)
 
-    def analyse(it):
+    def analyse(it, first=False):
         slabs = vall[it].reshape(NZ, NX, RB, 2 * ch)
         joined = jnp.concatenate(
             [slabs[:, q].reshape(NZ * RB, 2 * ch) for q in range(NX)], axis=1
         )
         high, low = split(joined)
         size = NZ * RB
-        main = mm(jnp.concatenate([high, low], axis=0), s8h[...])
-        product = main[:size] + main[size:] + mm(high, s8l[...])
+        stacked = jnp.concatenate([high, low], axis=0)
+        if first:
+            main = mm(stacked, s8th[...], ((1,), (1,)))
+            product = main[:size] + main[size:] + mm(high, s8tl[...], ((1,), (1,)))
+        else:
+            main = mm(stacked, s8h[...])
+            product = main[:size] + main[size:] + mm(high, s8l[...])
         image = product[0:RB]
         for k in range(1, NZ):
             image = image + pltpu.roll(product[k * RB:(k + 1) * RB], width - 2 * NX * k, 1)
         return image
+
+    def whole_tile():
+        return jnp.concatenate(
+            [
+                jnp.concatenate([halo[1, g], sb[0, g], sb[1, g], halo[0, g]], axis=1)
+                for g in range(NY)
+            ],
+            axis=0,
+        )
+
+    def setup_rows():
+        full = whole_tile()
+        for shift in range(2 * NX):
+            moved = full if shift == 0 else pltpu.roll(full, width - shift, 1)
+            high, low = split(moved)
+            s8h[shift * ch:(shift + 1) * ch, :] = high
+            s8l[shift * ch:(shift + 1) * ch, :] = low
 
     def setup_tile():
         for cc, yy, i in tile_in:
@@ -207,19 +229,7 @@
         for s in range(2):
             for dy in range(NY):
                 arrived(halo.at[s, plus(y, NY - dy, NY)], halo_base[s * NY + dy])
-        full = jnp.concatenate(
-            [
-                jnp.concatenate([halo[1, g], sb[0, g], sb[1, g], halo[0, g]], axis=1)
-                for g in range(NY)
-            ],
-            axis=0,
-        )
-        for shift in range(2 * NX):
-            moved = full if shift == 0 else pltpu.roll(full, width - shift, 1)
-            high, low = split(moved)
-            s8h[shift * ch:(shift + 1) * ch, :] = high
-            s8l[shift * ch:(shift + 1) * ch, :] = low
-        turned[0:width, :] = full.T
+        turned[0:width, :] = whole_tile().T
         turned[width:width + 8, :] = jnp.zeros((8, ch), F32)
         for shift in range(2 * NX):
             high, low = split(turned[shift:shift + width, :])
@@ -369,7 +379,8 @@
     gather_relay(moving, order)
     setup_tile()
     gather_finish(moving)
-    folding = normal_start(0, analyse(0))
+    folding = normal_start(0, analyse(0, True))
+    setup_rows()
     for o in range(NZ):
         normal_relay(folding, o)
     chunk = normal_finish(folding)
@@ -433,7 +444,10 @@
     fac[0] = inverse.T
     weights = exact(fac[0, pl.ds(pl.multiple_of(y * 2 * RB, 2 * RB), 2 * RB), :], inverse)
     shared(joined)
-    image = exact(weights, yx[...].reshape(rank, span))
+    high, low = split(weights)
+    wide_high, wide_low = split(yx[...].reshape(rank, span))
+    main = mm(jnp.concatenate([high, low], axis=0), wide_high)
+    image = main[:2 * RB] + main[2 * RB:] + mm(high, wide_low)
     for i in range(tiles):
         high, low = split(image if i == 0 else pltpu.roll(image, 2 * i, 1))
         yh[i * 2 * RB:(i + 1) * 2 * RB, :] = high

time: 102 us -> 103 us (level)
  no operation moved by 1% of the time
where the time goes in v7:
time: 103 us
  Pallas kernels  101 us (98%)
  local copies, waits for them, and re-layouts  1.24 us (1%)
    pallas_call x1, Pallas kernels, shards(): pl.pallas_call(kernel, out_shape=(jax.ShapeDtypeStruct((CHG, HALF), F32),...  101 us

profile of v7, /device:TPU:1, one launch (start us, length us, event | category | flops | bytes accessed | tf_op | source)
XLA Modules:
  0.0 103.1 jit_solution(16809705554146585358)
XLA Ops:
  0.6 101.2 %shard_map.50 = (f32[32,512]{1,0:T(8,128)S(1)}, f32[32,128]{1,0:T(8,128)S(1)}) custom-call(f32[32,512]{1,0:T(8,128)} %ks_hbm.1, s32[32,512]{1,0:T(8,128)} %mask_hbm.1, f32[32,128]{1,0:T(8,128)} %bitcast.3), custom_call_target="tpu_custom_call" | custom-call | tf_op jit(solution)/shard_map/pallas_call | solution.py:491
  101.8 0.6 copy.7
  102.5 0.6 copy.8

commit v8 on v6

--- a/solution.py
+++ b/solution.py
@@ -433,7 +433,10 @@
     fac[0] = inverse.T
     weights = exact(fac[0, pl.ds(pl.multiple_of(y * 2 * RB, 2 * RB), 2 * RB), :], inverse)
     shared(joined)
-    image = exact(weights, yx[...].reshape(rank, span))
+    high, low = split(weights)
+    wide_high, wide_low = split(yx[...].reshape(rank, span))
+    main = mm(jnp.concatenate([high, low], axis=0), wide_high)
+    image = main[:2 * RB] + main[2 * RB:] + mm(high, wide_low)
     for i in range(tiles):
         high, low = split(image if i == 0 else pltpu.roll(image, 2 * i, 1))
         yh[i * 2 * RB:(i + 1) * 2 * RB, :] = high

time: 102 us -> 102 us (level)
  no operation moved by 1% of the time
where the time goes in v8:
time: 102 us
  Pallas kernels  100 us (98%)
  local copies, waits for them, and re-layouts  1.24 us (1%)
    pallas_call x1, Pallas kernels, shards(): pl.pallas_call(kernel, out_shape=(jax.ShapeDtypeStruct((CHG, HALF), F32),...  100 us

profile of v8, /device:TPU:1, one launch (start us, length us, event | category | flops | bytes accessed | tf_op | source)
XLA Modules:
  0.0 102.1 jit_solution(15989798427278984531)
XLA Ops:
  0.6 100.2 %shard_map.50 = (f32[32,512]{1,0:T(8,128)S(1)}, f32[32,128]{1,0:T(8,128)S(1)}) custom-call(f32[32,512]{1,0:T(8,128)} %ks_hbm.1, s32[32,512]{1,0:T(8,128)} %mask_hbm.1, f32[32,128]{1,0:T(8,128)} %bitcast.3), custom_call_target="tpu_custom_call" | custom-call | tf_op jit(solution)/shard_map/pallas_call | solution.py:480
  100.9 0.6 copy.7
  101.5 0.6 copy.8
